TPU v7x, 256 devices: a whole 4x4x8 slice. The times are simulated.
256 devices in a mesh: bus: 32 (over x, z), case: 8 (over y, core).
Axes of the slice: x: 4, y: 4, z: 8, core: 2. Of those that a mesh axis runs over, the one named last changes fastest.
Arguments:
- z_columns: float32 [32768, 1024], P('bus')
- resident_bus: int32 [1024], replicated, may hold values from 0 to 32767, as said below
- fault_col: int32 [4096], P('case'), may hold values from 0 to 1023
- switch_cols: int32 [4096, 2], P('case'), may hold values from 0 to 1023, as said below
- tie_x: float32 [4096], P('case'), may hold values from 0.5 to 2
- fault_z: float32 [4096], P('case'), may hold values from 0.5 to 2
- boundary_send: int32 [32, 2, 128], replicated, may hold values from 0 to 1023, as said below
- branch_ends: int32 [49152, 2], P('bus'), may hold values from 0 to 1279, as said below
- branch_x: float32 [49152], P('bus'), may hold values from 0.01 to 0.05
- pickup: float32 [49152], P('bus'), may hold values from 0.2 to 1.5
- tds: float32 [49152], P('bus'), may hold values from 0.05 to 0.5
- curve: int32 [49152], P('bus'), may hold values from 0 to 2
Outputs:
- voltage: float32 [32768, 4096], P('bus', 'case')
- relay_rate: float32 [49152, 4096], P('bus', 'case')
- worst_rate: float32 [49152], P('bus')
Inputs may be any that keep to these rules, and one draw needn't show every extreme that they name: `resident_bus`: distinct bus ids. `switch_cols`: the two columns of a case differ. `boundary_send`: rows sent to the lower block lie among the first 256 rows, rows sent to the upper block among the last 256; each block's live slots come first and hold distinct rows, padding repeats the first slot's row; the first block sends nothing down and the last nothing up; some block fills all 128 slots. `branch_ends`: a to slot of 1024 or more points at a live slot of the neighbour's block; the first block never uses the lower slots, the last never the upper ones; a local to row differs from the from row.
All inputs are finite; a program needn't handle non-finite values.
Results may differ from a plain program's by a relative error of at most 0.000049.
Values sent between devices are 32-bit elements; how exact they have to be, the bound alone decides.
A program may use at most 64 MiB of HBM per device.

v0:
```python
import jax
import jax.numpy as jnp
from jax import lax
from jax.sharding import PartitionSpec as P


def shifted(value, axis, by):
    size = lax.axis_size(axis)
    pairs = [(i, i + by) for i in range(size) if 0 <= i + by < size]
    return lax.ppermute(value, axis, pairs)


def relay_of(currents, pickup, tds, curve):
    factor = jnp.where(curve == 0, 0.14, jnp.where(curve == 1, 13.5, 80.0)).astype(jnp.float32)
    exponent = jnp.where(curve == 0, 0.02, jnp.where(curve == 1, 1.0, 2.0)).astype(jnp.float32)
    scaled = currents / pickup[:, None]
    powered = jnp.exp(0.5 * exponent[:, None] * jnp.log(scaled * scaled + 0.0001))
    return jnp.maximum(powered - 1.0, 0.0) / (factor * tds)[:, None]


def per_device(
    z_columns,
    resident_bus,
    fault_col,
    switch_cols,
    tie_x,
    fault_z,
    boundary_send,
    branch_ends,
    branch_x,
    pickup,
    tds,
    curve,
):
    rows_dev = z_columns.shape[0]
    my_index = lax.axis_index("bus")
    fault_cols = jnp.take(z_columns, fault_col, axis=1)
    branch_diff = jnp.take(z_columns, switch_cols[:, 0], axis=1) - jnp.take(
        z_columns, switch_cols[:, 1], axis=1
    )
    offset = my_index * rows_dev
    row_a = jnp.take(resident_bus, switch_cols[:, 0]) - offset
    row_b = jnp.take(resident_bus, switch_cols[:, 1]) - offset
    row_f = jnp.take(resident_bus, fault_col) - offset
    row_ids = lax.broadcasted_iota(jnp.int32, (rows_dev, 1), 0)

    def pick_rows(column, wanted):
        return jnp.sum(jnp.where(row_ids == wanted[None, :], column, 0.0), axis=0)

    partial_value = jnp.stack(
        [
            pick_rows(branch_diff, row_a) - pick_rows(branch_diff, row_b),
            pick_rows(branch_diff, row_f),
            pick_rows(fault_cols, row_f),
        ]
    )
    own_lists = lax.dynamic_index_in_dim(boundary_send, my_index, 0, keepdims=False)
    entry_sums = lax.psum(partial_value, "bus")
    weight_ratio = entry_sums[1] / (tie_x + entry_sums[0])
    self_z = entry_sums[2] - entry_sums[1] * weight_ratio
    fault_amps = 1.0 / (self_z + fault_z)
    voltage = 1.0 - (fault_cols - branch_diff * weight_ratio[None, :]) * fault_amps[None, :]
    fields = voltage[None]
    going_down = jnp.take(fields, own_lists[0], axis=1)
    going_up = jnp.take(fields, own_lists[1], axis=1)
    from_lower = shifted(going_up, "bus", 1)
    from_upper = shifted(going_down, "bus", -1)
    extended = jnp.concatenate([fields, from_lower, from_upper], axis=1)[0]
    drops = jnp.take(extended, branch_ends[:, 0], axis=0) - jnp.take(
        extended, branch_ends[:, 1], axis=0
    )
    currents = drops / branch_x[:, None]
    relay_rate = relay_of(currents, pickup, tds, curve)
    worst_rate = lax.pmax(jnp.max(relay_rate, axis=1), "case")
    return (voltage, relay_rate, worst_rate)


def solution(mesh):
    in_specs = (
        P("bus", None),
        P(),
        P("case"),
        P("case", None),
        P("case"),
        P("case"),
        P(),
        P("bus", None),
        P("bus"),
        P("bus"),
        P("bus"),
        P("bus"),
    )
    out_specs = (P("bus", "case"), P("bus", "case"), P("bus"))
    return jax.shard_map(
        per_device, mesh=mesh, in_specs=in_specs, out_specs=out_specs, check_vma=False
    )
```

profile of v0, /device:TPU:1, one launch (start us, length us, event | category | flops | bytes accessed | tf_op | source)
XLA Modules:
  0.0 166.8 jit_solution(13267739268833994264)
XLA Ops:
  0.6 0.0 copy-start
  0.6 0.0 copy-start.1
  0.7 0.8 fusion.11
  1.5 3.4 %gather_fusion.4 = s32[512]{0:T(512)S(1)} fusion(s32[1024]{0:T(1024)} %param.21, s32[1024]{0:T(1024)S(1)} %pad_clamp_fusion.4), kind=kCustom, calls=%fused_computation.6.clone | custom fusion | bytes 6144 | tf_op jit(solution)/shard_map/jit(_take)/gather | solution.py:43
  4.8 0.0 copy-done.1
  4.8 2.3 %gather_fusion.3 = s32[512]{0:T(512)S(1)} fusion(s32[1024]{0:T(1024)S(1)} %copy-done.1, s32[1024]{0:T(1024)S(1)} %pad_clamp_fusion.5), kind=kCustom, calls=%fused_computation.1.clone | custom fusion | bytes 6144 | tf_op jit(solution)/shard_map/jit(_take)/gather | solution.py:42
  7.1 5.4 %copy.25 = f32[1024,1024]{0,1:T(8,128)} copy(f32[1024,1024]{1,0:T(8,128)} %param.20) | data formatting | bytes 8388608 | tf_op args[0]
  12.5 5.8 %gather_fusion.1 = f32[512,1024]{1,0:T(8,128)} fusion(f32[1024,1024]{0,1:T(8,128)} %copy.25, s32[1024]{0:T(1024)S(1)} %pad_clamp_fusion.5), kind=kCustom, calls=%fused_computation.4.clone | custom fusion | bytes 4196352 | tf_op jit(solution)/shard_map/jit(_take)/gather | solution.py:38
  18.3 0.0 copy-start.6
  18.3 5.8 %gather_fusion.2 = f32[512,1024]{1,0:T(8,128)} fusion(f32[1024,1024]{0,1:T(8,128)} %copy.25, s32[1024]{0:T(1024)S(1)} %pad_clamp_fusion.4), kind=kCustom, calls=%fused_computation.5.clone | custom fusion | bytes 4196352 | tf_op jit(solution)/shard_map/jit(_take)/gather | solution.py:38
  24.1 0.0 copy-done.6
  24.1 2.3 %gather_fusion.5 = s32[512]{0:T(512)S(1)} fusion(s32[1024]{0:T(1024)S(1)} %copy-done.1, s32[1024]{0:T(1024)S(1)} %pad_clamp_fusion.6), kind=kCustom, calls=%fused_computation.7.clone | custom fusion | bytes 6144 | tf_op jit(solution)/shard_map/jit(_take)/gather | solution.py:44
  26.4 5.0 %gather_fusion = f32[512,1024]{1,0:T(8,128)S(1)} fusion(f32[1024,1024]{0,1:T(8,128)} %copy.25, s32[1024]{0:T(1024)S(1)} %pad_clamp_fusion.6), kind=kCustom, calls=%fused_computation.clone | custom fusion | bytes 4196352 | tf_op jit(solution)/shard_map/jit(_take)/gather | solution.py:37
  31.5 0.0 copy-start.9
  31.5 0.0 copy-start.10
  31.5 4.2 %select_reduce_fusion.1 = (f32[512]{0:T(512)S(1)}, f32[512]{0:T(512)S(1)}, f32[512]{0:T(512)S(1)}, f32[512]{0:T(512)S(1)}, f32[1024,512]{0,1:T(8,128)}) fusion(s32[512]{0:T(512)S(1)} %get-tuple-element.44, s32[512]{0:T(512)S(1)} %get-tuple-element.33, s32[512]{0:T(512)S(1)} %get-tuple-element.31, f32[512,1024]{1,0:T(8,128)S(1)} %gather_fusion, ...), kind=kLoop, calls=%fused_computation.27 | loop fusion | flops 7862272 | bytes 8404480 | tf_op jit(solution)/shard_map/reduce_sum | solution.py:48
  35.7 65.3 %psum.7 = f32[3,512]{1,0:T(4,128)S(1)} all-reduce(f32[3,512]{1,0:T(4,128)S(1)} %pad_maximum_fusion), channel_id=1, replica_groups=mesh['bus'=32,'case'=8] {'bus'}, use_global_device_ids=true, to_apply=%region_4.7 | all-reduce | flops 1536 | bytes 12288 | tf_op jit(solution)/shard_map/psum | solution.py:58
  101.1 0.0 copy-done.9
  101.1 0.0 copy-done.10
  101.1 3.4 %fusion.8 = f32[1024,512]{0,1:T(8,128)} fusion(f32[1024,512]{0,1:T(8,128)} %get-tuple-element.30, f32[512,1024]{1,0:T(8,128)S(1)} %gather_fusion, f32[512]{0:T(512)S(1)} %get-tuple-element.28, f32[512]{0:T(512)S(1)} %get-tuple-element.29, pred[512]{0:T(512)(128)(4,1)S(1)} %get-tuple-element.34), kind=kLoop, calls=%fused_computation.24 | loop fusion | flops 2621440 | bytes 6296064 | tf_op jit(solution)/shard_map/sub | solution.py:62
  104.5 1.9 %copy.34 = f32[1024,512]{1,0:T(8,128)S(1)} copy(f32[1024,512]{0,1:T(8,128)} %fusion.8) | data formatting | bytes 4194304
  106.4 0.0 copy-start.2
  106.5 0.0 copy-done
  106.5 0.8 gather_fusion.6
  107.3 0.1 copy.29
  107.4 0.0 copy-start.3
  107.4 0.0 copy-start.7
  107.4 0.0 copy-start.4
  107.4 0.0 copy-start.5
  107.5 0.0 copy-start.8
  107.5 1.3 collective-permute-start
  108.8 0.8 gather_fusion.7
  109.6 0.0 copy-done.2
  109.6 0.1 copy.31
  109.7 1.3 collective-permute-start.1
  111.0 0.0 copy-done.3
  111.1 0.0 copy-done.7
  111.2 0.0 copy-done.4
  111.2 0.0 copy-done.5
  111.2 0.0 copy-done.8
  111.2 0.9 collective-permute-done
  112.2 4.7 %collective-permute-done.1 = f32[1,128,512]{1,2,0:T(8,128)S(1)} collective-permute-done((f32[1,128,512]{1,2,0:T(8,128)S(1)}, f32[1,128,512]{1,2,0:T(8,128)S(1)}, u32[]{:S(2)}, u32[]{:S(2)}) %collective-permute-start.1) | collective-permute-done | bytes 262176 | tf_op jit(solution)/shard_map/ppermute | solution.py:10
  116.9 3.3 %maximum_bitcast_fusion = f32[1280,512]{0,1:T(8,128)} fusion(f32[1,128,512]{1,2,0:T(8,128)S(1)} %collective-permute-done.1, f32[1,128,512]{1,2,0:T(8,128)S(1)} %collective-permute-done, f32[1,1024,512]{1,2,0:T(8,128)} %bitcast.36), kind=kLoop, calls=%fused_computation.18 | loop fusion | flops 1310720 | bytes 5242880 | tf_op jit(solution)/shard_map/squeeze | solution.py:68
  120.2 2.1 %copy.32 = f32[1280,512]{1,0:T(8,128)S(1)} copy(f32[1280,512]{0,1:T(8,128)} %maximum_bitcast_fusion) | data formatting | bytes 5242880 | tf_op jit(solution)/shard_map/squeeze | solution.py:68
  122.3 5.0 %gather_fusion.8 = f32[1536,512]{1,0:T(8,128)} fusion(f32[1280,512]{1,0:T(8,128)S(1)} %copy.32, s32[2048]{0:T(1024)S(1)} %pad_clamp_fusion.1), kind=kCustom, calls=%fused_computation.3.clone | custom fusion | bytes 6297600 | tf_op jit(solution)/shard_map/jit(_take)/gather | solution.py:69
  127.3 4.9 %gather_fusion.9 = f32[1536,512]{1,0:T(8,128)} fusion(f32[1280,512]{1,0:T(8,128)S(1)} %copy.32, s32[2048]{0:T(1024)S(1)} %pad_clamp_fusion), kind=kCustom, calls=%fused_computation.9.clone | custom fusion | bytes 6297600 | tf_op jit(solution)/shard_map/jit(_take)/gather | solution.py:69
  132.2 5.9 %fusion.9 = (f32[1536]{0:T(1024)S(1)}, f32[1536,512]{1,0:T(8,128)}) fusion(f32[1536]{0:T(1024)S(1)} %select_multiply_fusion, f32[1536]{0:T(1024)S(1)} %multiply.4, f32[1536,512]{1,0:T(8,128)} %gather_fusion.9, pred[1536]{0:T(1024)(128)(4,1)S(1)} %get-tuple-element.48, f32[1536,512]{1,0:T(8,128)} %gather_fusion.8, pred[1536]{0:T(1024)(128)(4,1)S(1)} %get-tuple-element.49, ...), kind=kLoop, calls=%fused_computation.67 | loop fusion | flops 8649216 | bytes 9464832 | tf_op jit(solution)/shard_map/reduce_max | solution.py:74
  138.1 28.7 %pmax.7 = f32[1536]{0:T(1024)} all-reduce(f32[1536]{0:T(1024)S(1)} %get-tuple-element.19), channel_id=1, replica_groups=mesh['bus'=32,'case'=8] {'case'}, use_global_device_ids=true, to_apply=%region_6.11 | all-reduce | flops 1536 | bytes 12288 | tf_op jit(solution)/shard_map/pmax | solution.py:74
  (26 shorter events, 0.3 us)
Async XLA Ops:
  0.6 105.8 %copy-start = (s32[32,2,128]{2,1,0:T(2,128)S(1)}, s32[32,2,128]{2,1,0:T(2,128)}, u32[]{:S(2)}) copy-start(s32[32,2,128]{2,1,0:T(2,128)} %param.26) | copy-start | bytes 98308
  0.6 4.2 %copy-start.1 = (s32[1024]{0:T(1024)S(1)}, s32[1024]{0:T(1024)}, u32[]{:S(2)}) copy-start(s32[1024]{0:T(1024)} %param.21) | copy-start | bytes 12292
  18.3 5.8 %copy-start.6 = (s32[512]{0:T(512)S(1)}, s32[512]{0:T(512)}, u32[]{:S(2)}) copy-start(s32[512]{0:T(512)} %param.22) | copy-start | bytes 6148
  31.5 69.6 %copy-start.9 = (f32[512]{0:T(512)S(1)}, f32[512]{0:T(512)}, u32[]{:S(2)}) copy-start(f32[512]{0:T(512)} %param.25) | copy-start | bytes 6148
  31.5 69.6 %copy-start.10 = (f32[512]{0:T(512)S(1)}, f32[512]{0:T(512)}, u32[]{:S(2)}) copy-start(f32[512]{0:T(512)} %param.24) | copy-start | bytes 6148
  106.4 3.1 %copy-start.2 = (f32[1024,512]{1,0:T(8,128)}, f32[1024,512]{1,0:T(8,128)S(1)}, u32[]{:S(2)}) copy-start(f32[1024,512]{1,0:T(8,128)S(1)} %copy.34) | copy-start | bytes 6291460
  107.4 3.6 %copy-start.3 = (s32[1536,2]{0,1:T(2,128)S(1)}, s32[1536,2]{0,1:T(2,128)}, u32[]{:S(2)}) copy-start(s32[1536,2]{0,1:T(2,128)} %param.27) | copy-start | bytes 36868
  107.4 3.7 %copy-start.7 = (s32[1536]{0:T(1024)S(1)}, s32[1536]{0:T(1024)}, u32[]{:S(2)}) copy-start(s32[1536]{0:T(1024)} %param.31) | copy-start | bytes 18436
  107.4 3.8 %copy-start.4 = (f32[1536]{0:T(1024)S(1)}, f32[1536]{0:T(1024)}, u32[]{:S(2)}) copy-start(f32[1536]{0:T(1024)} %param.28) | copy-start | bytes 18436
  107.4 3.8 %copy-start.5 = (f32[1536]{0:T(1024)S(1)}, f32[1536]{0:T(1024)}, u32[]{:S(2)}) copy-start(f32[1536]{0:T(1024)} %param.29) | copy-start | bytes 18436
  107.5 3.8 %copy-start.8 = (f32[1536]{0:T(1024)S(1)}, f32[1536]{0:T(1024)}, u32[]{:S(2)}) copy-start(f32[1536]{0:T(1024)} %param.30) | copy-start | bytes 18436
  107.5 4.7 %collective-permute-start = (f32[1,128,512]{1,2,0:T(8,128)S(1)}, f32[1,128,512]{1,2,0:T(8,128)S(1)}, u32[]{:S(2)}, u32[]{:S(2)}) collective-permute-start(f32[1,128,512]{1,2,0:T(8,128)S(1)} %bitcast_select_fusion.2), channel_id=1, source_target_pairs={{0,8},{8,16},{16,24},{24,32},{32,40},{40,48},{48,56},{56,64},{64,7... | collective-permute-start | bytes 786440 | tf_op jit(solution)/shard_map/ppermute | solution.py:10
  109.7 7.1 %collective-permute-start.1 = (f32[1,128,512]{1,2,0:T(8,128)S(1)}, f32[1,128,512]{1,2,0:T(8,128)S(1)}, u32[]{:S(2)}, u32[]{:S(2)}) collective-permute-start(f32[1,128,512]{1,2,0:T(8,128)S(1)} %bitcast_select_fusion.1), channel_id=1, source_target_pairs={{8,0},{16,8},{24,16},{32,24},{40,32},{48,40},{56,48},{64,56},{72,6... | collective-permute-start | bytes 786440 | tf_op jit(solution)/shard_map/ppermute | solution.py:10
where the time goes:
time: 167 us
  blocking collectives  94.1 us (56%)
  local copies, waits for them, and re-layouts  46.5 us (28%)
  other arithmetic  17 us (10%)
  waiting for transfers between devices  5.62 us (3%)
  starting transfers between devices  2.6 us (2%)
    psum x1, blocking collectives, per_device(): entry_sums = lax.psum(partial_value, 'bus')  65.3 us
    pmax x1, blocking collectives, per_device(): worst_rate = lax.pmax(jnp.max(relay_rate, axis=1), 'case')  28.7 us
    unnamed x24, local copies, waits for them, and re-layouts  7.35 us
    reduce_max x1, other arithmetic, per_device(): worst_rate = lax.pmax(jnp.max(relay_rate, axis=1), 'case')  5.9 us
    gather x1, local copies, waits for them, and re-layouts, per_device(): jnp.take(z_columns, switch_cols[:, 1], axis=1)  5.8 us
    gather x1, local copies, waits for them, and re-layouts, per_device(): jnp.take(z_columns, switch_cols[:, 0], axis=1)  5.78 us
    ppermute x2, waiting for transfers between devices, shifted(): return lax.ppermute(value, axis, pairs)  5.62 us
    gather x1, local copies, waits for them, and re-layouts, per_device(): fault_cols = jnp.take(z_columns, fault_col, axis=1)  5.01 us
  transfers between devices with their start and end apart: 2, of which 2 were waited for; matrix products, arithmetic and copies ran while one was open for 1% of the time, Pallas kernels for 0%

commit v1 on v0

v1 whole, which is shorter than its diff:
```python
import functools

import jax
import jax.numpy as jnp
from jax import lax
from jax.experimental import pallas as pl
from jax.experimental.pallas import tpu as pltpu
from jax.sharding import PartitionSpec as P

MESH = pl.DeviceIdType.MESH
F32, BF16, I32 = jnp.float32, jnp.bfloat16, jnp.int32
BUS, COLS, CASE, BR, HB, RIM = 1024, 1024, 512, 1536, 128, 256
CHUNK = 256
MIB = 1 << 20


def pieces(value):
    high = value.astype(BF16)
    rest = value - high.astype(F32)
    middle = rest.astype(BF16)
    low = (rest - middle.astype(F32)).astype(BF16)
    return high, middle, low


def onehot(mask):
    return jnp.where(mask, 1.0, 0.0)


def voltage_kernel(
    n_x,
    n_z,
    z_hbm,
    resident_ref,
    fault_ref,
    switch_ref,
    tie_ref,
    fault_z_ref,
    lists_ref,
    volt_ref,
    z_ref,
    select_ref,
    cols_ref,
    rows_out,
    rows_in,
    part_ref,
    total_ref,
    x_in,
    z_in,
    load_sem,
    halo_send,
    halo_recv,
    x_send,
    x_recv,
    z_send,
    z_recv,
):
    n_bus = n_x * n_z
    bus = lax.axis_index("bus")
    my_x, my_z = bus // n_z, bus % n_z
    upper, lower = (bus + 1) % n_bus, (bus + n_bus - 1) % n_bus
    x_peers = [((my_x + d) % n_x) * n_z + my_z for d in range(1, n_x)]
    z_peers = [my_x * n_z + (my_z + d) % n_z for d in range(1, n_z)]

    loads = []
    for i in range(BUS // CHUNK):
        rows = pl.ds(i * CHUNK, CHUNK)
        loads.append(pltpu.make_async_copy(z_hbm.at[rows], z_ref.at[rows], load_sem.at[i]))
    for i in (0, 3, 1, 2):
        loads[i].start()

    barrier = pltpu.get_barrier_semaphore()
    peers = [upper, lower] + x_peers + z_peers
    for peer in peers:
        pl.semaphore_signal(barrier, inc=1, device_id={"bus": peer}, device_id_type=MESH)

    fault = fault_ref[...]
    first, second = switch_ref[0:1, :], switch_ref[1:2, :]

    def build(i, carry):
        k = lax.broadcasted_iota(I32, (CHUNK, CASE), 0) + i * CHUNK
        rows = pl.ds(pl.multiple_of(i * CHUNK, CHUNK), CHUNK)
        select_ref[rows, 0:CASE] = onehot(k == fault).astype(BF16)
        select_ref[rows, CASE:] = (onehot(k == first) - onehot(k == second)).astype(BF16)
        return carry

    lax.fori_loop(0, COLS // CHUNK, build, 0)

    lists = lists_ref[bus]
    rim_ids = lax.broadcasted_iota(I32, (RIM, HB), 0)

    def boundary(side, start):
        chosen = onehot(rim_ids + start == lists[side : side + 1, :]).astype(BF16)
        total = None
        for piece in pieces(z_ref[start : start + RIM, :]):
            term = lax.dot_general(
                chosen, piece, (((0,), (0,)), ((), ())), preferred_element_type=F32
            )
            total = term if total is None else total + term
        rows_out[side] = total

    loads[0].wait()
    boundary(0, 0)
    loads[3].wait()
    boundary(1, BUS - RIM)
    pl.semaphore_wait(barrier, len(peers))

    def remote(src, dst, send, recv, peer):
        return pltpu.make_async_remote_copy(
            src_ref=src,
            dst_ref=dst,
            send_sem=send,
            recv_sem=recv,
            device_id={"bus": peer},
            device_id_type=MESH,
        )

    halo = [
        remote(rows_out.at[1], rows_in.at[0], halo_send.at[0], halo_recv.at[0], upper),
        remote(rows_out.at[0], rows_in.at[1], halo_send.at[1], halo_recv.at[1], lower),
    ]
    for copy in halo:
        copy.start()
    loads[1].wait()
    loads[2].wait()

    local = resident_ref[...] - bus * BUS
    column_ids = lax.broadcasted_iota(I32, (1, COLS), 1).astype(F32)
    first_f, second_f, fault_f = first.astype(F32), second.astype(F32), fault.astype(F32)

    def columns_of(value):
        stacked = jnp.concatenate(pieces(value), axis=0)
        got = jnp.dot(stacked, select_ref[...], preferred_element_type=F32)
        n = value.shape[0]
        return (got[:n] + got[n : 2 * n]) + got[2 * n :]

    def gather(i, sums):
        g1, g2, g3 = sums
        rows = pl.ds(pl.multiple_of(i * CHUNK, CHUNK), CHUNK)
        got = columns_of(z_ref[rows, :])
        cols_ref[rows, :] = got
        faults, diff = got[:, :CASE], got[:, CASE:]
        ids = lax.broadcasted_iota(I32, (CHUNK, COLS), 0) + i * CHUNK
        owner = jnp.max(jnp.where(ids == local, column_ids, -1.0), axis=1, keepdims=True)
        is_fault = owner == fault_f
        g1 = g1 + jnp.sum(
            jnp.where(owner == first_f, diff, jnp.where(owner == second_f, -diff, 0.0)),
            axis=0,
            keepdims=True,
        )
        g2 = g2 + jnp.sum(jnp.where(is_fault, diff, 0.0), axis=0, keepdims=True)
        g3 = g3 + jnp.sum(jnp.where(is_fault, faults, 0.0), axis=0, keepdims=True)
        return g1, g2, g3

    zero = jnp.zeros((1, CASE), F32)
    sums = lax.fori_loop(0, BUS // CHUNK, gather, (zero, zero, zero))
    for i in range(3):
        part_ref[:, i * CASE : (i + 1) * CASE] = sums[i]

    x_copies = [
        remote(part_ref, x_in.at[d], x_send.at[d], x_recv.at[d], x_peers[d]) for d in range(n_x - 1)
    ]
    for copy in x_copies:
        copy.start()
    for copy in x_copies:
        copy.wait_recv()
    total = part_ref[...]
    for d in range(n_x - 1):
        total = total + x_in[d]
    total_ref[...] = total
    z_copies = [
        remote(total_ref, z_in.at[d], z_send.at[d], z_recv.at[d], z_peers[d]) for d in range(n_z - 1)
    ]
    for copy in z_copies:
        copy.start()
    for copy in halo:
        copy.wait_recv()

    def gather_halo(i, carry):
        cols_ref[pl.ds(pl.multiple_of(BUS + i * HB, HB), HB), :] = columns_of(rows_in[i])
        return carry

    lax.fori_loop(0, 2, gather_halo, 0)
    for copy in z_copies:
        copy.wait_recv()
    for d in range(n_z - 1):
        total = total + z_in[d]
    g1, g2, g3 = total[:, :CASE], total[:, CASE : 2 * CASE], total[:, 2 * CASE :]
    ratio = g2 / (tie_ref[...] + g1)
    self_z = g3 - g2 * ratio
    amps = 1.0 / (self_z + fault_z_ref[...])

    def finish(i, carry):
        rows = pl.ds(pl.multiple_of(i * HB, HB), HB)
        got = cols_ref[rows, :]
        volt_ref[rows, :] = 1.0 - (got[:, :CASE] - got[:, CASE:] * ratio) * amps
        return carry

    lax.fori_loop(0, (BUS + 2 * HB) // HB, finish, 0)
    for copy in halo + x_copies + z_copies:
        copy.wait_send()


def voltages(n_x, n_z, z_columns, resident, fault, switch, tie_x, fault_z, lists):
    vmem = pl.BlockSpec(memory_space=pltpu.VMEM)
    dma = pltpu.SemaphoreType.DMA
    return pl.pallas_call(
        functools.partial(voltage_kernel, n_x, n_z),
        out_shape=jax.ShapeDtypeStruct((BUS + 2 * HB, CASE), F32),
        in_specs=[pl.BlockSpec(memory_space=pl.ANY)] + [vmem] * 6,
        out_specs=vmem,
        scratch_shapes=[
            pltpu.VMEM((BUS, COLS), F32),
            pltpu.VMEM((COLS, 2 * CASE), BF16),
            pltpu.VMEM((BUS + 2 * HB, 2 * CASE), F32),
            pltpu.VMEM((2, HB, COLS), F32),
            pltpu.VMEM((2, HB, COLS), F32),
            pltpu.VMEM((1, 3 * CASE), F32),
            pltpu.VMEM((1, 3 * CASE), F32),
            pltpu.VMEM((n_x - 1, 1, 3 * CASE), F32),
            pltpu.VMEM((n_z - 1, 1, 3 * CASE), F32),
            dma((BUS // CHUNK,)),
            dma((2,)),
            dma((2,)),
            dma((n_x - 1,)),
            dma((n_x - 1,)),
            dma((n_z - 1,)),
            dma((n_z - 1,)),
        ],
        compiler_params=pltpu.CompilerParams(
            collective_id=0, has_side_effects=True, vmem_limit_bytes=48 * MIB
        ),
        name="voltages",
    )(z_columns, resident, fault, switch, tie_x, fault_z, lists)


STEP = 512


def relay_kernel(volt_ref, ends_ref, x_ref, pickup_ref, tds_ref, curve_ref, volt_hbm, rate_ref, worst_ref, v_ref, par_ref, sem):
    step = pl.program_id(0)
    copy = pltpu.make_async_copy(volt_ref.at[pl.ds(0, BUS)], volt_hbm, sem)

    @pl.when(step == 0)
    def _():
        copy.start()

        def split(i, carry):
            rows = pl.ds(pl.multiple_of(i * HB, HB), HB)
            for j, piece in enumerate(pieces(volt_ref[rows, :])):
                v_ref[rows, j * CASE : (j + 1) * CASE] = piece
            return carry

        lax.fori_loop(0, (BUS + 2 * HB) // HB, split, 0)
        curve = curve_ref[...]
        factor = jnp.where(curve == 0, 0.14, jnp.where(curve == 1, 13.5, 80.0))
        half = jnp.where(curve == 0, 0.01, jnp.where(curve == 1, 0.5, 1.0))
        ends = ends_ref[...].astype(F32)
        rows = [
            ends[0:1],
            ends[1:2],
            1.0 / (x_ref[...] * pickup_ref[...]),
            half,
            1.0 / (factor * tds_ref[...]),
        ]
        rows = jnp.concatenate(rows + [jnp.zeros((3, BR), F32)], axis=0)
        par_ref[...] = rows.T

    branches = pl.ds(pl.multiple_of(step * STEP, STEP), STEP)
    par = par_ref[branches, :]
    ids = lax.broadcasted_iota(I32, (STEP, BUS + 2 * HB), 1)
    start, end = par[:, 0:1].astype(I32), par[:, 1:2].astype(I32)
    signs = (onehot(ids == start) - onehot(ids == end)).astype(BF16)
    got = jnp.dot(signs, v_ref[...], preferred_element_type=F32)
    drops = (got[:, :CASE] + got[:, CASE : 2 * CASE]) + got[:, 2 * CASE :]
    scaled = drops * par[:, 2:3]
    powered = jnp.exp(par[:, 3:4] * jnp.log(scaled * scaled + 0.0001))
    rate = jnp.maximum(powered - 1.0, 0.0) * par[:, 4:5]
    rate_ref[...] = rate
    tops = rate[:, 0:128]
    for j in range(1, CASE // 128):
        tops = jnp.maximum(tops, rate[:, j * 128 : (j + 1) * 128])
    worst_ref[...] = jnp.max(tops.T, axis=0, keepdims=True)

    @pl.when(step == BR // STEP - 1)
    def _():
        copy.wait()


def relays(volt, ends, branch_x, pickup, tds, curve):
    vmem = pl.BlockSpec(memory_space=pltpu.VMEM)
    return pl.pallas_call(
        relay_kernel,
        grid=(BR // STEP,),
        out_shape=(
            jax.ShapeDtypeStruct((BUS, CASE), F32),
            jax.ShapeDtypeStruct((BR, CASE), F32),
            jax.ShapeDtypeStruct((1, BR), F32),
        ),
        in_specs=[vmem] * 6,
        out_specs=(
            pl.BlockSpec(memory_space=pl.ANY),
            pl.BlockSpec((STEP, CASE), lambda i: (i, 0)),
            pl.BlockSpec((1, STEP), lambda i: (0, i)),
        ),
        scratch_shapes=[
            pltpu.VMEM((BUS + 2 * HB, 3 * CASE), BF16),
            pltpu.VMEM((BR, 8), F32),
            pltpu.SemaphoreType.DMA,
        ],
        compiler_params=pltpu.CompilerParams(
            dimension_semantics=("arbitrary",), vmem_limit_bytes=40 * MIB
        ),
        name="relays",
    )(volt, ends, branch_x, pickup, tds, curve)


def worst_kernel(n, mine_ref, out_ref, slots, send, recv):
    case = lax.axis_index("case")
    peers = [(case + d) % n for d in range(1, n)]
    barrier = pltpu.get_barrier_semaphore()
    for peer in peers:
        pl.semaphore_signal(barrier, inc=1, device_id={"case": peer}, device_id_type=MESH)
    pl.semaphore_wait(barrier, n - 1)
    copies = [
        pltpu.make_async_remote_copy(
            src_ref=mine_ref,
            dst_ref=slots.at[d],
            send_sem=send.at[d],
            recv_sem=recv.at[d],
            device_id={"case": peers[d]},
            device_id_type=MESH,
        )
        for d in range(n - 1)
    ]
    for copy in copies:
        copy.start()
    best = mine_ref[...]
    for d in range(n - 1):
        copies[d].wait_recv()
        best = jnp.maximum(best, slots[d])
    out_ref[...] = best
    for copy in copies:
        copy.wait_send()


def worst_over_cases(mine):
    n = lax.axis_size("case")
    vmem = pl.BlockSpec(memory_space=pltpu.VMEM)
    return pl.pallas_call(
        functools.partial(worst_kernel, n),
        out_shape=jax.ShapeDtypeStruct((1, BR), F32),
        in_specs=[vmem],
        out_specs=vmem,
        scratch_shapes=[
            pltpu.VMEM((n - 1, 1, BR), F32),
            pltpu.SemaphoreType.DMA((n - 1,)),
            pltpu.SemaphoreType.DMA((n - 1,)),
        ],
        compiler_params=pltpu.CompilerParams(collective_id=1, has_side_effects=True),
        name="worst",
    )(mine)


def per_device(
    z_columns,
    resident_bus,
    fault_col,
    switch_cols,
    tie_x,
    fault_z,
    boundary_send,
    branch_ends,
    branch_x,
    pickup,
    tds,
    curve,
):
    n_bus = lax.axis_size("bus")
    n_z = 8 if n_bus % 8 == 0 else 2
    row = lambda a: a.reshape(1, -1)
    volt = voltages(
        n_bus // n_z,
        n_z,
        z_columns,
        row(resident_bus),
        row(fault_col),
        switch_cols.T,
        row(tie_x),
        row(fault_z),
        boundary_send,
    )
    voltage, rate, worst = relays(
        volt, branch_ends.T, row(branch_x), row(pickup), row(tds), row(curve)
    )
    return voltage, rate, worst_over_cases(worst).reshape(BR)


def solution(mesh):
    in_specs = (
        P("bus", None),
        P(),
        P("case"),
        P("case", None),
        P("case"),
        P("case"),
        P(),
        P("bus", None),
        P("bus"),
        P("bus"),
        P("bus"),
        P("bus"),
    )
    out_specs = (P("bus", "case"), P("bus", "case"), P("bus"))
    return jax.shard_map(
        per_device, mesh=mesh, in_specs=in_specs, out_specs=out_specs, check_vma=False
    )
```

time: 167 us -> 54.3 us (0.33)
  blocking collectives: 94.1 us -> 0 us
  Pallas kernels: 0 us -> 44.2 us
  local copies, waits for them, and re-layouts: 46.5 us -> 7.57 us
  other arithmetic: 17 us -> 1.31 us
  waiting for transfers between devices: 5.62 us -> 0 us
  starting transfers between devices: 2.6 us -> 0 us
    psum x1 -> x0, blocking collectives: 65.3 us -> none  [per_device(): entry_sums = lax.psum(partial_value, 'bus')]
    pallas_call x0 -> x3, Pallas kernels: none -> 44.2 us  [the longest x1 26.2 us: voltages(): pl.pallas_call(functools.partial(voltage_kernel, n_x, n_z), out_shape=jax...]
    gather x12 -> x0, local copies, waits for them, and re-layouts: 36.2 us -> none  [the longest x1 5.8 us: per_device(): jnp.take(z_columns, switch_cols[:, 1], axis=1)]
    pmax x1 -> x0, blocking collectives: 28.7 us -> none  [per_device(): worst_rate = lax.pmax(jnp.max(relay_rate, axis=1), 'case')]
    reduce_max x1 -> x0, other arithmetic: 5.9 us -> none  [per_device(): worst_rate = lax.pmax(jnp.max(relay_rate, axis=1), 'case')]
    ppermute x2 -> x0, waiting for transfers between devices: 5.62 us -> none  [shifted(): return lax.ppermute(value, axis, pairs)]
    reduce_sum x1 -> x0, other arithmetic: 4.22 us -> none  [pick_rows(): return jnp.sum(jnp.where(row_ids == wanted[None, :], column, 0.0), axis=0)]
    sub x4 -> x0, other arithmetic: 3.43 us -> none  [the longest x1 3.4 us: per_device(): 1.0 - (fault_cols - branch_diff * weight_ratio[None, :]) * fault_amps[Non...]
  transfers between devices with their start and end apart: 2 -> 0, of which waited for: 2 -> 0; matrix products, arithmetic and copies ran while one was open for 1% -> 0% of each run, Pallas kernels for 0% -> 0%
where the time goes in v1:
time: 54.3 us; the launch traced here: 53.7 us
  Pallas kernels  44.2 us (81%)
  local copies, waits for them, and re-layouts  7.57 us (14%)
  other arithmetic  1.31 us (2%)
  between operations  0.68 us (1%)
    pallas_call x1, Pallas kernels, voltages(): pl.pallas_call(functools.partial(voltage_kernel, n_x, n_z), out_shape=jax...  26.2 us
    pallas_call x1, Pallas kernels, relays(): pl.pallas_call(relay_kernel, grid=(BR // STEP,), out_shape=(jax.ShapeDtyp...  10 us
    pallas_call x1, Pallas kernels, worst_over_cases(): pl.pallas_call(functools.partial(worst_kernel, n), out_shape=jax.ShapeDty...  7.96 us
    unnamed x16, local copies, waits for them, and re-layouts  4.76 us
    reshape x4, local copies, waits for them, and re-layouts, per_device(): row = lambda a: a.reshape(1, -1)  2.81 us
    pallas_call x1, other arithmetic, worst_over_cases(): pl.pallas_call(functools.partial(worst_kernel, n), out_shape=jax.ShapeDty...  1.31 us

profile of v1, /device:TPU:1, one launch (start us, length us, event | category | flops | bytes accessed | tf_op | source)
XLA Modules:
  0.0 53.7 jit_solution(9221571810687364696)
XLA Ops:
  0.6 0.7 %reshape.37.x_ref = f32[1,1536]{1,0:T(1,128)S(1)} reshape(f32[1536]{0:T(1024)} %param.20) | data formatting | bytes 12288 | tf_op jit(solution)/shard_map/reshape | solution.py:380
  1.3 0.7 %reshape.38.pickup_ref = f32[1,1536]{1,0:T(1,128)S(1)} reshape(f32[1536]{0:T(1024)} %param.21) | data formatting | bytes 12288 | tf_op jit(solution)/shard_map/reshape | solution.py:380
  2.0 0.7 %reshape.39.tds_ref = f32[1,1536]{1,0:T(1,128)S(1)} reshape(f32[1536]{0:T(1024)} %param.22) | data formatting | bytes 12288 | tf_op jit(solution)/shard_map/reshape | solution.py:380
  2.7 0.7 %reshape.40.curve_ref = s32[1,1536]{1,0:T(1,128)S(1)} reshape(s32[1536]{0:T(1024)} %param.23) | data formatting | bytes 12288 | tf_op jit(solution)/shard_map/reshape | solution.py:380
  3.4 0.0 copy-start
  3.4 0.8 %copy-done = s32[32,2,128]{2,1,0:T(2,128)S(1)} copy-done((s32[32,2,128]{2,1,0:T(2,128)S(1)}, s32[32,2,128]{2,1,0:T(2,128)}, u32[]{:S(2)}) %copy-start) | copy-done | bytes 32792
  4.2 0.0 copy-start.3
  4.2 0.7 %copy-done.3 = s32[1024]{0:T(1024)S(1)} copy-done((s32[1024]{0:T(1024)S(1)}, s32[1024]{0:T(1024)}, u32[]{:S(2)}) %copy-start.3) | copy-done | bytes 4120
  4.9 0.0 copy-start.4
  4.9 0.7 %copy-done.4 = s32[512,2]{0,1:T(2,128)S(1)} copy-done((s32[512,2]{0,1:T(2,128)S(1)}, s32[512,2]{0,1:T(2,128)}, u32[]{:S(2)}) %copy-start.4) | copy-done | bytes 4120
  5.6 0.0 copy-start.5
  5.6 0.7 %copy-done.5 = s32[512]{0:T(512)S(1)} copy-done((s32[512]{0:T(512)S(1)}, s32[512]{0:T(512)}, u32[]{:S(2)}) %copy-start.5) | copy-done | bytes 2072
  6.3 0.0 copy-start.6
  6.3 0.7 %copy-done.6 = f32[512]{0:T(512)S(1)} copy-done((f32[512]{0:T(512)S(1)}, f32[512]{0:T(512)}, u32[]{:S(2)}) %copy-start.6) | copy-done | bytes 2072
  6.9 0.0 copy-start.7
  6.9 0.7 %copy-done.7 = f32[512]{0:T(512)S(1)} copy-done((f32[512]{0:T(512)S(1)}, f32[512]{0:T(512)}, u32[]{:S(2)}) %copy-start.7) | copy-done | bytes 2072
  7.6 0.0 copy-start.1
  7.6 26.2 %voltages.1.volt_ref = f32[1280,512]{1,0:T(8,128)S(1)} custom-call(f32[1024,1024]{1,0:T(8,128)} %z_hbm.1, s32[1,1024]{1,0:T(1,128)S(1)} %bitcast.7, s32[1,512]{1,0:T(1,128)S(1)} %bitcast.9, s32[2,512]{1,0:T(2,128)S(1)} %bitcast.8, f32[1,512]{1,0:T(1,128)S(1)} %bitcast.10, f32[1,512]{1,0:T(1,128)S(1)} %bitcast.11, s32[32,2,128]{2,1,0:T(2,128)S(1)} %copy-done), custom_call_target="tpu_custom_call" | custom-call | tf_op jit(solution)/shard_map/voltages/pallas_call | solution.py:206
  33.8 0.0 copy-done.1
  33.8 10.0 %relays.1 = (f32[1024,512]{1,0:T(8,128)}, f32[1536,512]{1,0:T(8,128)}, f32[1,1536]{1,0:T(1,128)S(1)}) custom-call(f32[1280,512]{1,0:T(8,128)S(1)} %voltages.1.volt_ref, s32[2,1536]{1,0:T(2,128)S(1)} %bitcast.6, f32[1,1536]{1,0:T(1,128)S(1)} %reshape.37.x_ref, f32[1,1536]{1,0:T(1,128)S(1)} %reshape.38.pickup_ref, f32[1,1536]{1,0:T(1,128)S(1)} %reshape.39.tds_ref, ...), custom_call_target="tpu_custom_call" | custom-call | tf_op jit(solution)/shard_map/relays/pallas_call | solution.py:291
  43.9 0.0 copy-start.2
  43.9 0.6 %copy-done.2 = f32[1,1536]{1,0:T(1,128)} copy-done((f32[1,1536]{1,0:T(1,128)}, f32[1,1536]{1,0:T(1,128)S(1)}, u32[]{:S(2)}) %copy-start.2) | copy-done | bytes 6168
  44.4 8.0 %worst.1 = f32[1,1536]{1,0:T(1,128)} custom-call(f32[1,1536]{1,0:T(1,128)} %copy-done.2), custom_call_target="tpu_custom_call" | custom-call | tf_op jit(solution)/shard_map/worst/pallas_call | solution.py:349
  52.4 1.3 %reduce = f32[1536]{0:T(1024)} reduce(f32[1,1536]{1,0:T(1,128)} %worst.1, f32[]{:T(128)} %constant), dimensions={0}, to_apply=%pallas_call.17.reduce_sub_computation | reduce | bytes 12292 | tf_op jit(solution)/shard_map/worst/pallas_call | solution.py:349
Async XLA Ops:
  3.4 0.8 %copy-start = (s32[32,2,128]{2,1,0:T(2,128)S(1)}, s32[32,2,128]{2,1,0:T(2,128)}, u32[]{:S(2)}) copy-start(s32[32,2,128]{2,1,0:T(2,128)} %lists_ref.1) | copy-start | bytes 98308
  4.2 0.7 %copy-start.3 = (s32[1024]{0:T(1024)S(1)}, s32[1024]{0:T(1024)}, u32[]{:S(2)}) copy-start(s32[1024]{0:T(1024)} %param.13) | copy-start | bytes 12292
  4.9 0.7 %copy-start.4 = (s32[512,2]{0,1:T(2,128)S(1)}, s32[512,2]{0,1:T(2,128)}, u32[]{:S(2)}) copy-start(s32[512,2]{0,1:T(2,128)} %param.15) | copy-start | bytes 12292
  5.6 0.7 %copy-start.5 = (s32[512]{0:T(512)S(1)}, s32[512]{0:T(512)}, u32[]{:S(2)}) copy-start(s32[512]{0:T(512)} %param.14) | copy-start | bytes 6148
  6.3 0.7 %copy-start.6 = (f32[512]{0:T(512)S(1)}, f32[512]{0:T(512)}, u32[]{:S(2)}) copy-start(f32[512]{0:T(512)} %param.16) | copy-start | bytes 6148
  6.9 0.7 %copy-start.7 = (f32[512]{0:T(512)S(1)}, f32[512]{0:T(512)}, u32[]{:S(2)}) copy-start(f32[512]{0:T(512)} %param.17) | copy-start | bytes 6148
  7.6 26.2 %copy-start.1 = (s32[1536,2]{0,1:T(2,128)S(1)}, s32[1536,2]{0,1:T(2,128)}, u32[]{:S(2)}) copy-start(s32[1536,2]{0,1:T(2,128)} %param.19) | copy-start | bytes 36868
  43.9 0.6 %copy-start.2 = (f32[1,1536]{1,0:T(1,128)}, f32[1,1536]{1,0:T(1,128)S(1)}, u32[]{:S(2)}) copy-start(f32[1,1536]{1,0:T(1,128)S(1)} %get-tuple-element.8.mine_ref) | copy-start | bytes 18436

commit v2 on v1

--- a/solution.py
+++ b/solution.py
@@ -22,6 +22,10 @@
     return high, middle, low
 
 
+def in_hbm(value):
+    return pltpu.with_memory_space_constraint(value, pltpu.HBM)
+
+
 def onehot(mask):
     return jnp.where(mask, 1.0, 0.0)
 
@@ -30,13 +34,19 @@
     n_x,
     n_z,
     z_hbm,
+    resident_hbm,
+    fault_hbm,
+    switch_hbm,
+    tie_hbm,
+    fault_z_hbm,
+    lists_hbm,
+    volt_ref,
     resident_ref,
     fault_ref,
     switch_ref,
     tie_ref,
     fault_z_ref,
     lists_ref,
-    volt_ref,
     z_ref,
     select_ref,
     cols_ref,
@@ -46,6 +56,7 @@
     total_ref,
     x_in,
     z_in,
+    small_sem,
     load_sem,
     halo_send,
     halo_recv,
@@ -61,6 +72,19 @@
     x_peers = [((my_x + d) % n_x) * n_z + my_z for d in range(1, n_x)]
     z_peers = [my_x * n_z + (my_z + d) % n_z for d in range(1, n_z)]
 
+    small = [
+        (fault_hbm, fault_ref),
+        (switch_hbm, switch_ref),
+        (lists_hbm.at[bus], lists_ref),
+        (resident_hbm, resident_ref),
+        (tie_hbm, tie_ref),
+        (fault_z_hbm, fault_z_ref),
+    ]
+    small = [
+        pltpu.make_async_copy(src, dst, small_sem.at[i]) for i, (src, dst) in enumerate(small)
+    ]
+    for copy in small:
+        copy.start()
     loads = []
     for i in range(BUS // CHUNK):
         rows = pl.ds(i * CHUNK, CHUNK)
@@ -73,6 +97,8 @@
     for peer in peers:
         pl.semaphore_signal(barrier, inc=1, device_id={"bus": peer}, device_id_type=MESH)
 
+    for copy in small:
+        copy.wait()
     fault = fault_ref[...]
     first, second = switch_ref[0:1, :], switch_ref[1:2, :]
 
@@ -85,7 +111,7 @@
 
     lax.fori_loop(0, COLS // CHUNK, build, 0)
 
-    lists = lists_ref[bus]
+    lists = lists_ref[...]
     rim_ids = lax.broadcasted_iota(I32, (RIM, HB), 0)
 
     def boundary(side, start):
@@ -206,9 +232,15 @@
     return pl.pallas_call(
         functools.partial(voltage_kernel, n_x, n_z),
         out_shape=jax.ShapeDtypeStruct((BUS + 2 * HB, CASE), F32),
-        in_specs=[pl.BlockSpec(memory_space=pl.ANY)] + [vmem] * 6,
+        in_specs=[pl.BlockSpec(memory_space=pltpu.HBM)] * 7,
         out_specs=vmem,
         scratch_shapes=[
+            pltpu.VMEM((1, COLS), I32),
+            pltpu.VMEM((1, CASE), I32),
+            pltpu.VMEM((2, CASE), I32),
+            pltpu.VMEM((1, CASE), F32),
+            pltpu.VMEM((1, CASE), F32),
+            pltpu.VMEM((2, HB), I32),
             pltpu.VMEM((BUS, COLS), F32),
             pltpu.VMEM((COLS, 2 * CASE), BF16),
             pltpu.VMEM((BUS + 2 * HB, 2 * CASE), F32),
@@ -218,6 +250,7 @@
             pltpu.VMEM((1, 3 * CASE), F32),
             pltpu.VMEM((n_x - 1, 1, 3 * CASE), F32),
             pltpu.VMEM((n_z - 1, 1, 3 * CASE), F32),
+            dma((6,)),
             dma((BUS // CHUNK,)),
             dma((2,)),
             dma((2,)),
@@ -230,19 +263,50 @@
             collective_id=0, has_side_effects=True, vmem_limit_bytes=48 * MIB
         ),
         name="voltages",
-    )(z_columns, resident, fault, switch, tie_x, fault_z, lists)
+    )(*map(in_hbm, (z_columns, resident, fault, switch, tie_x, fault_z, lists)))
 
 
 STEP = 512
 
 
-def relay_kernel(volt_ref, ends_ref, x_ref, pickup_ref, tds_ref, curve_ref, volt_hbm, rate_ref, worst_ref, v_ref, par_ref, sem):
+def relay_kernel(
+    volt_ref,
+    ends_hbm,
+    x_hbm,
+    pickup_hbm,
+    tds_hbm,
+    curve_hbm,
+    volt_hbm,
+    rate_ref,
+    worst_ref,
+    v_ref,
+    par_ref,
+    ends_ref,
+    x_ref,
+    pickup_ref,
+    tds_ref,
+    curve_ref,
+    sem,
+    small_sem,
+):
     step = pl.program_id(0)
     copy = pltpu.make_async_copy(volt_ref.at[pl.ds(0, BUS)], volt_hbm, sem)
 
     @pl.when(step == 0)
     def _():
         copy.start()
+        small = [
+            (ends_hbm, ends_ref),
+            (x_hbm, x_ref),
+            (pickup_hbm, pickup_ref),
+            (tds_hbm, tds_ref),
+            (curve_hbm, curve_ref),
+        ]
+        small = [
+            pltpu.make_async_copy(src, dst, small_sem.at[i]) for i, (src, dst) in enumerate(small)
+        ]
+        for load in small:
+            load.start()
 
         def split(i, carry):
             rows = pl.ds(pl.multiple_of(i * HB, HB), HB)
@@ -251,16 +315,19 @@
             return carry
 
         lax.fori_loop(0, (BUS + 2 * HB) // HB, split, 0)
-        curve = curve_ref[...]
+        for load in small:
+            load.wait()
+        row = lambda ref: ref[...].reshape(1, BR)
+        curve = row(curve_ref)
         factor = jnp.where(curve == 0, 0.14, jnp.where(curve == 1, 13.5, 80.0))
         half = jnp.where(curve == 0, 0.01, jnp.where(curve == 1, 0.5, 1.0))
         ends = ends_ref[...].astype(F32)
         rows = [
             ends[0:1],
             ends[1:2],
-            1.0 / (x_ref[...] * pickup_ref[...]),
+            1.0 / (row(x_ref) * row(pickup_ref)),
             half,
-            1.0 / (factor * tds_ref[...]),
+            1.0 / (factor * row(tds_ref)),
         ]
         rows = jnp.concatenate(rows + [jnp.zeros((3, BR), F32)], axis=0)
         par_ref[...] = rows.T
@@ -279,7 +346,9 @@
     tops = rate[:, 0:128]
     for j in range(1, CASE // 128):
         tops = jnp.maximum(tops, rate[:, j * 128 : (j + 1) * 128])
-    worst_ref[...] = jnp.max(tops.T, axis=0, keepdims=True)
+    for j in range(STEP // 128):
+        block = tops[j * 128 : (j + 1) * 128].T
+        worst_ref[pl.ds(step * (STEP // 128) + j, 1), :] = jnp.max(block, axis=0, keepdims=True)
 
     @pl.when(step == BR // STEP - 1)
     def _():
@@ -294,24 +363,30 @@
         out_shape=(
             jax.ShapeDtypeStruct((BUS, CASE), F32),
             jax.ShapeDtypeStruct((BR, CASE), F32),
-            jax.ShapeDtypeStruct((1, BR), F32),
+            jax.ShapeDtypeStruct((BR // 128, 128), F32),
         ),
-        in_specs=[vmem] * 6,
+        in_specs=[vmem] + [pl.BlockSpec(memory_space=pltpu.HBM)] * 5,
         out_specs=(
-            pl.BlockSpec(memory_space=pl.ANY),
+            pl.BlockSpec(memory_space=pltpu.HBM),
             pl.BlockSpec((STEP, CASE), lambda i: (i, 0)),
-            pl.BlockSpec((1, STEP), lambda i: (0, i)),
+            pl.BlockSpec((BR // 128, 128), lambda i: (0, 0)),
         ),
         scratch_shapes=[
             pltpu.VMEM((BUS + 2 * HB, 3 * CASE), BF16),
             pltpu.VMEM((BR, 8), F32),
+            pltpu.VMEM((2, BR), I32),
+            pltpu.VMEM((BR,), F32),
+            pltpu.VMEM((BR,), F32),
+            pltpu.VMEM((BR,), F32),
+            pltpu.VMEM((BR,), I32),
             pltpu.SemaphoreType.DMA,
+            pltpu.SemaphoreType.DMA((5,)),
         ],
         compiler_params=pltpu.CompilerParams(
             dimension_semantics=("arbitrary",), vmem_limit_bytes=40 * MIB
         ),
         name="relays",
-    )(volt, ends, branch_x, pickup, tds, curve)
+    )(volt, *map(in_hbm, (ends, branch_x, pickup, tds, curve)))
 
 
 def worst_kernel(n, mine_ref, out_ref, slots, send, recv):
@@ -348,15 +423,17 @@
     vmem = pl.BlockSpec(memory_space=pltpu.VMEM)
     return pl.pallas_call(
         functools.partial(worst_kernel, n),
-        out_shape=jax.ShapeDtypeStruct((1, BR), F32),
+        out_shape=jax.ShapeDtypeStruct((BR // 128, 128), F32),
         in_specs=[vmem],
         out_specs=vmem,
         scratch_shapes=[
-            pltpu.VMEM((n - 1, 1, BR), F32),
+            pltpu.VMEM((n - 1, BR // 128, 128), F32),
             pltpu.SemaphoreType.DMA((n - 1,)),
             pltpu.SemaphoreType.DMA((n - 1,)),
         ],
-        compiler_params=pltpu.CompilerParams(collective_id=1, has_side_effects=True),
+        compiler_params=pltpu.CompilerParams(
+            collective_id=1, has_side_effects=True, vmem_limit_bytes=MIB
+        ),
         name="worst",
     )(mine)
 
@@ -390,7 +467,7 @@
         boundary_send,
     )
     voltage, rate, worst = relays(
-        volt, branch_ends.T, row(branch_x), row(pickup), row(tds), row(curve)
+        volt, branch_ends.T, branch_x, pickup, tds, curve
     )
     return voltage, rate, worst_over_cases(worst).reshape(BR)
 

time: 54.3 us -> 46 us (0.85)
  local copies, waits for them, and re-layouts: 7.57 us -> 0.6 us
  other arithmetic: 1.31 us -> 0 us
    unnamed x16 -> x1, local copies, waits for them, and re-layouts: 4.76 us -> 0.6 us
    reshape x4 -> x0, local copies, waits for them, and re-layouts: 2.81 us -> none  [per_device(): row = lambda a: a.reshape(1, -1)]
    pallas_call x1 -> x0, other arithmetic: 1.31 us -> none  [worst_over_cases(): pl.pallas_call(functools.partial(worst_kernel, n), out_shape=jax.ShapeDty...]
    pallas_call x1, Pallas kernels: 26.2 us -> 27.4 us  [voltages(): pl.pallas_call(functools.partial(voltage_kernel, n_x, n_z), out_shape=jax...]
    pallas_call x1, Pallas kernels: 7.96 us -> 6.87 us  [worst_over_cases(): pl.pallas_call(functools.partial(worst_kernel, n), out_shape=jax.ShapeDty...]
where the time goes in v2:
time: 46 us; the launch traced here: 45.8 us
  Pallas kernels  44.6 us (97%)
  between operations  0.66 us (1%)
  local copies, waits for them, and re-layouts  0.6 us (1%)
    pallas_call x1, Pallas kernels, voltages(): pl.pallas_call(functools.partial(voltage_kernel, n_x, n_z), out_shape=jax...  27.4 us
    pallas_call x1, Pallas kernels, relays(): pl.pallas_call(relay_kernel, grid=(BR // STEP,), out_shape=(jax.ShapeDtyp...  10.3 us
    pallas_call x1, Pallas kernels, worst_over_cases(): pl.pallas_call(functools.partial(worst_kernel, n), out_shape=jax.ShapeDty...  6.87 us

profile of v2, /device:TPU:1, one launch (start us, length us, event | category | flops | bytes accessed | tf_op | source)
XLA Modules:
  0.0 45.8 jit_solution(14763195128776055863)
XLA Ops:
  0.6 27.4 %voltages.1.volt_ref = f32[1280,512]{1,0:T(8,128)S(1)} custom-call(f32[1024,1024]{1,0:T(8,128)} %z_hbm.1, s32[1,1024]{1,0:T(1,128)} %bitcast.9, s32[1,512]{1,0:T(1,128)} %bitcast.11, s32[2,512]{1,0:T(2,128)} %bitcast.10, f32[1,512]{1,0:T(1,128)} %bitcast.12, f32[1,512]{1,0:T(1,128)} %bitcast.13, s32[32,2,128]{2,1,0:T(2,128)} %lists_hbm.1), custom_call_target="tpu_custom_call" | custom-call | tf_op jit(solution)/shard_map/voltages/pallas_call | solution.py:232
  28.1 10.3 %relays.1 = (f32[1024,512]{1,0:T(8,128)}, f32[1536,512]{1,0:T(8,128)}, f32[12,128]{1,0:T(8,128)S(1)}) custom-call(f32[1280,512]{1,0:T(8,128)S(1)} %voltages.1.volt_ref, s32[2,1536]{1,0:T(2,128)} %bitcast.8, f32[1536]{0:T(1024)} %x_hbm.1, f32[1536]{0:T(1024)} %pickup_hbm.1, f32[1536]{0:T(1024)} %tds_hbm.1, s32[1536]{0:T(1024)} %curve_hbm.1), custom_call_target="tpu_custom_call" | custom-call | tf_op jit(solution)/shard_map/relays/pallas_call | solution.py:360
  38.4 6.9 %worst.1 = f32[12,128]{1,0:T(8,128)S(1)} custom-call(f32[12,128]{1,0:T(8,128)S(1)} %get-tuple-element.8.mine_ref), custom_call_target="tpu_custom_call" | custom-call | tf_op jit(solution)/shard_map/worst/pallas_call | solution.py:424
  45.2 0.6 %copy.16 = f32[1536]{0:T(1024)} copy(f32[1536]{0:T(1024)S(1)} %bitcast.7) | data formatting | bytes 12288

commit v3 on v1

v3 whole, which is shorter than its diff:
```python
import functools

import jax
import jax.numpy as jnp
from jax import lax
from jax.experimental import pallas as pl
from jax.experimental.pallas import tpu as pltpu
from jax.sharding import PartitionSpec as P

MESH = pl.DeviceIdType.MESH
F32, BF16, I32 = jnp.float32, jnp.bfloat16, jnp.int32
BUS, COLS, CASE, BR, HB, RIM = 1024, 1024, 512, 1536, 128, 256
CHUNK = 256
EXT, HALF = BUS + 2 * HB, CASE // 2
MIB = 1 << 20


def pieces(value):
    high = value.astype(BF16)
    rest = value - high.astype(F32)
    middle = rest.astype(BF16)
    low = (rest - middle.astype(F32)).astype(BF16)
    return high, middle, low


def in_hbm(value):
    return pltpu.with_memory_space_constraint(value, pltpu.HBM)


def onehot(mask):
    return jnp.where(mask, 1.0, 0.0)


def relay_of(scaled, half, inverse):
    powered = jnp.exp(half * jnp.log(scaled * scaled + 0.0001))
    return jnp.maximum(powered - 1.0, 0.0) * inverse


def screen_kernel(
    n_x,
    n_z,
    n_case,
    z_hbm,
    resident_hbm,
    fault_hbm,
    switch_hbm,
    tie_hbm,
    fault_z_hbm,
    lists_hbm,
    ends_hbm,
    x_hbm,
    pickup_hbm,
    tds_hbm,
    curve_hbm,
    volt_ref,
    rate_ref,
    worst_ref,
    resident_ref,
    fault_ref,
    switch_ref,
    tie_ref,
    fault_z_ref,
    lists_ref,
    ends_ref,
    x_ref,
    pickup_ref,
    tds_ref,
    curve_ref,
    z_ref,
    select_ref,
    cols_ref,
    rows_out,
    rows_in,
    part_ref,
    total_ref,
    x_in,
    z_in,
    signs_ref,
    v_ref,
    par_ref,
    most_ref,
    most_in,
    small_sem,
    load_sem,
    halo_send,
    halo_recv,
    x_send,
    x_recv,
    z_send,
    z_recv,
    c_send,
    c_recv,
):
    n_bus = n_x * n_z
    bus, case = lax.axis_index("bus"), lax.axis_index("case")
    my_x, my_z = bus // n_z, bus % n_z
    upper, lower = (bus + 1) % n_bus, (bus + n_bus - 1) % n_bus
    x_peers = [((my_x + d) % n_x) * n_z + my_z for d in range(1, n_x)]
    z_peers = [my_x * n_z + (my_z + d) % n_z for d in range(1, n_z)]
    case_peers = [(case + d) % n_case for d in range(1, n_case)]

    small = [
        (fault_hbm, fault_ref),
        (switch_hbm, switch_ref),
        (lists_hbm.at[bus], lists_ref),
        (resident_hbm, resident_ref),
        (tie_hbm, tie_ref),
        (fault_z_hbm, fault_z_ref),
        (ends_hbm, ends_ref),
        (x_hbm, x_ref),
        (pickup_hbm, pickup_ref),
        (tds_hbm, tds_ref),
        (curve_hbm, curve_ref),
    ]
    small = [
        pltpu.make_async_copy(src, dst, small_sem.at[i]) for i, (src, dst) in enumerate(small)
    ]
    for copy in small[:4]:
        copy.start()
    loads = []
    for i in range(BUS // CHUNK):
        rows = pl.ds(i * CHUNK, CHUNK)
        loads.append(pltpu.make_async_copy(z_hbm.at[rows], z_ref.at[rows], load_sem.at[i]))
    for i in (0, 3, 1, 2):
        loads[i].start()
    for copy in small[4:]:
        copy.start()

    barrier = pltpu.get_barrier_semaphore()
    bus_peers = [upper, lower] + x_peers + z_peers
    for peer in bus_peers:
        pl.semaphore_signal(barrier, inc=1, device_id={"bus": peer}, device_id_type=MESH)
    for peer in case_peers:
        pl.semaphore_signal(barrier, inc=1, device_id={"case": peer}, device_id_type=MESH)

    for copy in small[:4]:
        copy.wait()
    fault = fault_ref[...]
    first, second = switch_ref[0:1, :], switch_ref[1:2, :]

    def build(i, carry):
        k = lax.broadcasted_iota(I32, (CHUNK, CASE), 0) + i * CHUNK
        rows = pl.ds(pl.multiple_of(i * CHUNK, CHUNK), CHUNK)
        select_ref[rows, 0:CASE] = onehot(k == fault).astype(BF16)
        select_ref[rows, CASE:] = (onehot(k == first) - onehot(k == second)).astype(BF16)
        return carry

    lax.fori_loop(0, COLS // CHUNK, build, 0)

    lists = lists_ref[...]
    rim_ids = lax.broadcasted_iota(I32, (RIM, HB), 0)

    def boundary(side, start):
        chosen = onehot(rim_ids + start == lists[side : side + 1, :]).astype(BF16)
        total = None
        for piece in pieces(z_ref[start : start + RIM, :]):
            term = lax.dot_general(
                chosen, piece, (((0,), (0,)), ((), ())), preferred_element_type=F32
            )
            total = term if total is None else total + term
        rows_out[side] = total

    loads[0].wait()
    boundary(0, 0)
    loads[3].wait()
    boundary(1, BUS - RIM)
    pl.semaphore_wait(barrier, len(bus_peers) + len(case_peers))

    def remote(src, dst, send, recv, axis, peer):
        return pltpu.make_async_remote_copy(
            src_ref=src,
            dst_ref=dst,
            send_sem=send,
            recv_sem=recv,
            device_id={axis: peer},
            device_id_type=MESH,
        )

    halo = [
        remote(rows_out.at[1], rows_in.at[0], halo_send.at[0], halo_recv.at[0], "bus", upper),
        remote(rows_out.at[0], rows_in.at[1], halo_send.at[1], halo_recv.at[1], "bus", lower),
    ]
    for copy in halo:
        copy.start()
    loads[1].wait()
    loads[2].wait()

    local = resident_ref[...] - bus * BUS
    column_ids = lax.broadcasted_iota(I32, (1, COLS), 1).astype(F32)
    first_f, second_f, fault_f = first.astype(F32), second.astype(F32), fault.astype(F32)

    def columns_of(value):
        stacked = jnp.concatenate(pieces(value), axis=0)
        got = jnp.dot(stacked, select_ref[...], preferred_element_type=F32)
        n = value.shape[0]
        return (got[:n] + got[n : 2 * n]) + got[2 * n :]

    def gather(i, sums):
        g1, g2, g3 = sums
        rows = pl.ds(pl.multiple_of(i * CHUNK, CHUNK), CHUNK)
        got = columns_of(z_ref[rows, :])
        cols_ref[rows, :] = got
        faults, diff = got[:, :CASE], got[:, CASE:]
        ids = lax.broadcasted_iota(I32, (CHUNK, COLS), 0) + i * CHUNK
        owner = jnp.max(jnp.where(ids == local, column_ids, -1.0), axis=1, keepdims=True)
        is_fault = owner == fault_f
        g1 = g1 + jnp.sum(
            jnp.where(owner == first_f, diff, jnp.where(owner == second_f, -diff, 0.0)),
            axis=0,
            keepdims=True,
        )
        g2 = g2 + jnp.sum(jnp.where(is_fault, diff, 0.0), axis=0, keepdims=True)
        g3 = g3 + jnp.sum(jnp.where(is_fault, faults, 0.0), axis=0, keepdims=True)
        return g1, g2, g3

    zero = jnp.zeros((1, CASE), F32)
    sums = lax.fori_loop(0, BUS // CHUNK, gather, (zero, zero, zero))
    for i in range(3):
        part_ref[:, i * CASE : (i + 1) * CASE] = sums[i]

    x_copies = [
        remote(part_ref, x_in.at[d], x_send.at[d], x_recv.at[d], "bus", x_peers[d])
        for d in range(n_x - 1)
    ]
    for copy in x_copies:
        copy.start()

    for copy in small[4:]:
        copy.wait()
    curve, tds = curve_ref[...], tds_ref[...]
    factor = jnp.where(curve == 0, 0.14, jnp.where(curve == 1, 13.5, 80.0))
    half = jnp.where(curve == 0, 0.01, jnp.where(curve == 1, 0.5, 1.0))
    scale = 1.0 / (x_ref[...] * pickup_ref[...])
    inverse = 1.0 / (factor * tds)

    def as_row(value):
        return jnp.concatenate([value[j : j + 1, :] for j in range(BR // 128)], axis=1)

    ends = ends_ref[...].astype(F32)
    rows = [ends[0:1], ends[1:2], as_row(scale), as_row(half), as_row(inverse)]
    rows = jnp.concatenate(rows + [jnp.zeros((3, BR), F32)], axis=0)
    par_ref[...] = rows.T

    def build_signs(i, carry):
        rows = pl.ds(pl.multiple_of(i * CHUNK, CHUNK), CHUNK)
        par = par_ref[rows, :]
        ids = lax.broadcasted_iota(I32, (CHUNK, EXT), 1)
        start, end = par[:, 0:1].astype(I32), par[:, 1:2].astype(I32)
        signs_ref[rows, :] = (onehot(ids == start) - onehot(ids == end)).astype(BF16)
        return carry

    lax.fori_loop(0, 3, build_signs, 0)
    for copy in x_copies:
        copy.wait_recv()
    total = part_ref[...]
    for d in range(n_x - 1):
        total = total + x_in[d]
    total_ref[...] = total
    z_copies = [
        remote(total_ref, z_in.at[d], z_send.at[d], z_recv.at[d], "bus", z_peers[d])
        for d in range(n_z - 1)
    ]
    for copy in z_copies:
        copy.start()
    lax.fori_loop(3, BR // CHUNK, build_signs, 0)
    for copy in halo:
        copy.wait_recv()

    def gather_halo(i, carry):
        cols_ref[pl.ds(pl.multiple_of(BUS + i * HB, HB), HB), :] = columns_of(rows_in[i])
        return carry

    lax.fori_loop(0, 2, gather_halo, 0)
    for copy in z_copies:
        copy.wait_recv()
    for d in range(n_z - 1):
        total = total + z_in[d]
    g1, g2, g3 = total[:, :CASE], total[:, CASE : 2 * CASE], total[:, 2 * CASE :]
    ratio = g2 / (tie_ref[...] + g1)
    self_z = g3 - g2 * ratio
    amps = 1.0 / (self_z + fault_z_ref[...])

    def finish(i, keep):
        rows = pl.ds(pl.multiple_of(i * HB, HB), HB)
        got = cols_ref[rows, :]
        volt = 1.0 - (got[:, :CASE] - got[:, CASE:] * ratio) * amps
        if keep:
            volt_ref[rows, :] = volt
        for j, piece in enumerate(pieces(volt)):
            for h in range(2):
                at = (h * 3 + j) * HALF
                v_ref[rows, at : at + HALF] = piece[:, h * HALF : (h + 1) * HALF]

    @pl.loop(0, BUS // HB)
    def _(i):
        finish(i, True)

    @pl.loop(BUS // HB, EXT // HB)
    def _(i):
        finish(i, False)

    for h in range(2):
        got = jnp.dot(
            signs_ref[...],
            v_ref[:, h * 3 * HALF : (h + 1) * 3 * HALF],
            preferred_element_type=F32,
        )
        rate_ref[:, h * HALF : (h + 1) * HALF] = (got[:, :HALF] + got[:, HALF : 2 * HALF]) + got[
            :, 2 * HALF :
        ]

    @pl.loop(0, BR // 128)
    def _(i):
        drops = jnp.abs(rate_ref[pl.ds(pl.multiple_of(i * 128, 128), 128), :])
        tops = drops[:, 0:128]
        for j in range(1, CASE // 128):
            tops = jnp.maximum(tops, drops[:, j * 128 : (j + 1) * 128])
        most_ref[pl.ds(i, 1), :] = jnp.max(tops.T, axis=0, keepdims=True)

    c_copies = [
        remote(most_ref, most_in.at[d], c_send.at[d], c_recv.at[d], "case", case_peers[d])
        for d in range(n_case - 1)
    ]
    for copy in c_copies:
        copy.start()

    @pl.loop(0, BR // 128)
    def _(i):
        rows = pl.ds(pl.multiple_of(i * 128, 128), 128)
        par = par_ref[rows, :]
        rate_ref[rows, :] = relay_of(rate_ref[rows, :] * par[:, 2:3], par[:, 3:4], par[:, 4:5])

    most = most_ref[...]
    for d in range(n_case - 1):
        c_copies[d].wait_recv()
        most = jnp.maximum(most, most_in[d])
    worst_ref[...] = relay_of(most * scale, half, inverse)
    for copy in halo + x_copies + z_copies + c_copies:
        copy.wait_send()


def store_kernel(volt_ref, rate_ref, worst_ref, volt_hbm, rate_hbm, worst_hbm, sem):
    pairs = [(volt_ref, volt_hbm), (rate_ref, rate_hbm), (worst_ref, worst_hbm)]
    copies = [pltpu.make_async_copy(src, dst, sem.at[i]) for i, (src, dst) in enumerate(pairs)]
    for copy in copies:
        copy.start()
    for copy in copies:
        copy.wait()


def per_device(
    z_columns,
    resident_bus,
    fault_col,
    switch_cols,
    tie_x,
    fault_z,
    boundary_send,
    branch_ends,
    branch_x,
    pickup,
    tds,
    curve,
):
    n_bus, n_case = lax.axis_size("bus"), lax.axis_size("case")
    n_z = 8 if n_bus % 8 == 0 else 2
    n_x = n_bus // n_z
    row = lambda a: a.reshape(1, -1)
    tiles = lambda a: a.reshape(-1, 128)
    operands = (
        z_columns,
        row(resident_bus),
        row(fault_col),
        switch_cols.T,
        row(tie_x),
        row(fault_z),
        boundary_send,
        branch_ends.T,
        tiles(branch_x),
        tiles(pickup),
        tiles(tds),
        tiles(curve),
    )
    vmem, hbm = pl.BlockSpec(memory_space=pltpu.VMEM), pl.BlockSpec(memory_space=pltpu.HBM)
    dma = pltpu.SemaphoreType.DMA
    shapes = (
        jax.ShapeDtypeStruct((BUS, CASE), F32),
        jax.ShapeDtypeStruct((BR, CASE), F32),
        jax.ShapeDtypeStruct((BR // 128, 128), F32),
    )
    results = pl.pallas_call(
        functools.partial(screen_kernel, n_x, n_z, n_case),
        out_shape=shapes,
        in_specs=[hbm] * len(operands),
        out_specs=(vmem,) * 3,
        scratch_shapes=[
            pltpu.VMEM((1, COLS), I32),
            pltpu.VMEM((1, CASE), I32),
            pltpu.VMEM((2, CASE), I32),
            pltpu.VMEM((1, CASE), F32),
            pltpu.VMEM((1, CASE), F32),
            pltpu.VMEM((2, HB), I32),
            pltpu.VMEM((2, BR), I32),
            pltpu.VMEM((BR // 128, 128), F32),
            pltpu.VMEM((BR // 128, 128), F32),
            pltpu.VMEM((BR // 128, 128), F32),
            pltpu.VMEM((BR // 128, 128), I32),
            pltpu.VMEM((BUS, COLS), F32),
            pltpu.VMEM((COLS, 2 * CASE), BF16),
            pltpu.VMEM((EXT, 2 * CASE), F32),
            pltpu.VMEM((2, HB, COLS), F32),
            pltpu.VMEM((2, HB, COLS), F32),
            pltpu.VMEM((1, 3 * CASE), F32),
            pltpu.VMEM((1, 3 * CASE), F32),
            pltpu.VMEM((n_x - 1, 1, 3 * CASE), F32),
            pltpu.VMEM((n_z - 1, 1, 3 * CASE), F32),
            pltpu.VMEM((BR, EXT), BF16),
            pltpu.VMEM((EXT, 3 * CASE), BF16),
            pltpu.VMEM((BR, 8), F32),
            pltpu.VMEM((BR // 128, 128), F32),
            pltpu.VMEM((n_case - 1, BR // 128, 128), F32),
            dma((11,)),
            dma((BUS // CHUNK,)),
            dma((2,)),
            dma((2,)),
            dma((n_x - 1,)),
            dma((n_x - 1,)),
            dma((n_z - 1,)),
            dma((n_z - 1,)),
            dma((n_case - 1,)),
            dma((n_case - 1,)),
        ],
        compiler_params=pltpu.CompilerParams(
            collective_id=0, has_side_effects=True, vmem_limit_bytes=44 * MIB
        ),
        name="screen",
    )(*map(in_hbm, operands))
    voltage, rate, worst = pl.pallas_call(
        store_kernel,
        out_shape=shapes,
        in_specs=[vmem] * 3,
        out_specs=(hbm,) * 3,
        scratch_shapes=[dma((3,))],
        compiler_params=pltpu.CompilerParams(vmem_limit_bytes=MIB),
        name="store",
    )(*results)
    return voltage, rate, worst.reshape(BR)


def solution(mesh):
    in_specs = (
        P("bus", None),
        P(),
        P("case"),
        P("case", None),
        P("case"),
        P("case"),
        P(),
        P("bus", None),
        P("bus"),
        P("bus"),
        P("bus"),
        P("bus"),
    )
    out_specs = (P("bus", "case"), P("bus", "case"), P("bus"))
    return jax.shard_map(
        per_device, mesh=mesh, in_specs=in_specs, out_specs=out_specs, check_vma=False
    )
```

time: 54.3 us -> 44.5 us (0.82)
  local copies, waits for them, and re-layouts: 7.57 us -> 0 us
  other arithmetic: 1.31 us -> 0 us
    unnamed x16 -> x0, local copies, waits for them, and re-layouts: 4.76 us -> none
    reshape x4 -> x0, local copies, waits for them, and re-layouts: 2.81 us -> none  [per_device(): row = lambda a: a.reshape(1, -1)]
    pallas_call x1 -> x0, other arithmetic: 1.31 us -> none  [worst_over_cases(): pl.pallas_call(functools.partial(worst_kernel, n), out_shape=jax.ShapeDty...]
    pallas_call x3 -> x2, Pallas kernels: 44.2 us -> 43.8 us  [the longest x1 41.4 us: per_device(): pl.pallas_call(functools.partial(screen_kernel, n_x, n_z, n_case), out_sh...]
where the time goes in v3:
time: 44.5 us; the launch traced here: 44.4 us
  Pallas kernels  43.8 us (98%)
  between operations  0.64 us (1%)
    pallas_call x1, Pallas kernels, per_device(): pl.pallas_call(functools.partial(screen_kernel, n_x, n_z, n_case), out_sh...  41.4 us
    pallas_call x1, Pallas kernels, per_device(): pl.pallas_call(store_kernel, out_shape=shapes, in_specs=[vmem] * 3, out_s...  2.38 us

profile of v3, /device:TPU:1, one launch (start us, length us, event | category | flops | bytes accessed | tf_op | source)
XLA Modules:
  0.0 44.4 jit_solution(15147126537886096715)
XLA Ops:
  0.6 41.4 %screen.1 = (f32[1024,512]{1,0:T(8,128)S(1)}, f32[1536,512]{1,0:T(8,128)S(1)}, f32[12,128]{1,0:T(8,128)S(1)}) custom-call(f32[1024,1024]{1,0:T(8,128)} %z_hbm.1, s32[1,1024]{1,0:T(1,128)} %bitcast.16, s32[1,512]{1,0:T(1,128)} %bitcast.18, s32[2,512]{1,0:T(2,128)} %bitcast.17, f32[1,512]{1,0:T(1,128)} %bitcast.19, f32[1,512]{1,0:T(1,128)} %bitcast.20, ...), custom_call_target="tpu_custom_call" | custom-call | tf_op jit(solution)/shard_map/screen/pallas_call | solution.py:391
  42.1 2.4 %store.1 = (f32[1024,512]{1,0:T(8,128)}, f32[1536,512]{1,0:T(8,128)}, f32[12,128]{1,0:T(8,128)}) custom-call(f32[1024,512]{1,0:T(8,128)S(1)} %get-tuple-element.9.volt_ref, f32[1536,512]{1,0:T(8,128)S(1)} %get-tuple-element.10.rate_ref, f32[12,128]{1,0:T(8,128)S(1)} %get-tuple-element.11.worst_ref), custom_call_target="tpu_custom_call" | custom-call | tf_op jit(solution)/shard_map/store/pallas_call | solution.py:438

commit v4 on v3

--- a/solution.py
+++ b/solution.py
@@ -11,7 +11,7 @@
 F32, BF16, I32 = jnp.float32, jnp.bfloat16, jnp.int32
 BUS, COLS, CASE, BR, HB, RIM = 1024, 1024, 512, 1536, 128, 256
 CHUNK = 256
-EXT, HALF = BUS + 2 * HB, CASE // 2
+EXT, HALF = BUS + 2 * HB, HB // 2
 MIB = 1 << 20
 
 
@@ -67,6 +67,7 @@
     tds_ref,
     curve_ref,
     z_ref,
+    cut_ref,
     select_ref,
     cols_ref,
     rows_out,
@@ -84,6 +85,8 @@
     load_sem,
     halo_send,
     halo_recv,
+    hand_send,
+    hand_recv,
     x_send,
     x_recv,
     z_send,
@@ -97,6 +100,8 @@
     upper, lower = (bus + 1) % n_bus, (bus + n_bus - 1) % n_bus
     x_peers = [((my_x + d) % n_x) * n_z + my_z for d in range(1, n_x)]
     z_peers = [my_x * n_z + (my_z + d) % n_z for d in range(1, n_z)]
+    core = case % 2
+    sibling = case + 1 - 2 * core
     case_peers = [(case + d) % n_case for d in range(1, n_case)]
 
     small = [
@@ -147,8 +152,8 @@
 
     lax.fori_loop(0, COLS // CHUNK, build, 0)
 
-    lists = lists_ref[...]
-    rim_ids = lax.broadcasted_iota(I32, (RIM, HB), 0)
+    lists = jnp.where(core == 0, lists_ref[:, :HALF], lists_ref[:, HALF:])
+    rim_ids = lax.broadcasted_iota(I32, (RIM, HALF), 0)
 
     def boundary(side, start):
         chosen = onehot(rim_ids + start == lists[side : side + 1, :]).astype(BF16)
@@ -160,12 +165,6 @@
             total = term if total is None else total + term
         rows_out[side] = total
 
-    loads[0].wait()
-    boundary(0, 0)
-    loads[3].wait()
-    boundary(1, BUS - RIM)
-    pl.semaphore_wait(barrier, len(bus_peers) + len(case_peers))
-
     def remote(src, dst, send, recv, axis, peer):
         return pltpu.make_async_remote_copy(
             src_ref=src,
@@ -176,47 +175,72 @@
             device_id_type=MESH,
         )
 
-    halo = [
-        remote(rows_out.at[1], rows_in.at[0], halo_send.at[0], halo_recv.at[0], "bus", upper),
-        remote(rows_out.at[0], rows_in.at[1], halo_send.at[1], halo_recv.at[1], "bus", lower),
-    ]
-    for copy in halo:
-        copy.start()
-    loads[1].wait()
-    loads[2].wait()
-
+    mine = pl.ds(pl.multiple_of(core * HALF, HALF), HALF)
+    halo, hand = [], []
+    for side, peer in ((0, upper), (1, lower)):
+        part = rows_in.at[side, mine]
+        halo.append(
+            remote(
+                rows_out.at[1 - side], part, halo_send.at[side], halo_recv.at[side], "bus", peer
+            )
+        )
+        hand.append(remote(part, part, hand_send.at[side], hand_recv.at[side], "case", sibling))
     local = resident_ref[...] - bus * BUS
     column_ids = lax.broadcasted_iota(I32, (1, COLS), 1).astype(F32)
     first_f, second_f, fault_f = first.astype(F32), second.astype(F32), fault.astype(F32)
 
-    def columns_of(value):
-        stacked = jnp.concatenate(pieces(value), axis=0)
-        got = jnp.dot(stacked, select_ref[...], preferred_element_type=F32)
-        n = value.shape[0]
-        return (got[:n] + got[n : 2 * n]) + got[2 * n :]
-
-    def gather(i, sums):
-        g1, g2, g3 = sums
-        rows = pl.ds(pl.multiple_of(i * CHUNK, CHUNK), CHUNK)
-        got = columns_of(z_ref[rows, :])
-        cols_ref[rows, :] = got
-        faults, diff = got[:, :CASE], got[:, CASE:]
+    def gather(values, select):
+        total = None
+        for value in values:
+            term = jnp.dot(value, select, preferred_element_type=F32)
+            total = term if total is None else total + term
+        return total
+
+    def switch_part(i, sums):
+        g1, g2, own = sums
+        rows = pl.ds(i * CHUNK, CHUNK)
+        z = z_ref[rows, :]
+        parts = pieces(z)
+        for j in range(3):
+            cut_ref[j, rows, :] = parts[j]
+        diff = gather(parts, select_ref[:, CASE:])
+        cols_ref[rows, CASE:] = diff
         ids = lax.broadcasted_iota(I32, (CHUNK, COLS), 0) + i * CHUNK
-        owner = jnp.max(jnp.where(ids == local, column_ids, -1.0), axis=1, keepdims=True)
-        is_fault = owner == fault_f
+        resident = ids == local
+        owner = jnp.max(jnp.where(resident, column_ids, -1.0), axis=1, keepdims=True)
         g1 = g1 + jnp.sum(
             jnp.where(owner == first_f, diff, jnp.where(owner == second_f, -diff, 0.0)),
             axis=0,
             keepdims=True,
         )
-        g2 = g2 + jnp.sum(jnp.where(is_fault, diff, 0.0), axis=0, keepdims=True)
-        g3 = g3 + jnp.sum(jnp.where(is_fault, faults, 0.0), axis=0, keepdims=True)
-        return g1, g2, g3
+        g2 = g2 + jnp.sum(jnp.where(owner == fault_f, diff, 0.0), axis=0, keepdims=True)
+        own = own + jnp.sum(jnp.where(resident, z, 0.0), axis=0, keepdims=True)
+        return g1, g2, own
+
+    def fault_part(i):
+        rows = pl.ds(i * CHUNK, CHUNK)
+        parts = [cut_ref[j, rows, :] for j in range(3)]
+        cols_ref[rows, :CASE] = gather(parts, select_ref[:, :CASE])
 
     zero = jnp.zeros((1, CASE), F32)
-    sums = lax.fori_loop(0, BUS // CHUNK, gather, (zero, zero, zero))
-    for i in range(3):
-        part_ref[:, i * CASE : (i + 1) * CASE] = sums[i]
+    sums = (zero, zero, jnp.zeros((1, COLS), F32))
+    loads[0].wait()
+    loads[3].wait()
+    boundary(0, 0)
+    boundary(1, BUS - RIM)
+    sums = switch_part(0, sums)
+    pl.semaphore_wait(barrier, len(bus_peers) + len(case_peers))
+    for copy in halo:
+        copy.start()
+    loads[1].wait()
+    loads[2].wait()
+    for i in (3, 1, 2):
+        sums = switch_part(i, sums)
+    g1, g2, own = sums
+    parts = pieces(jnp.broadcast_to(own, (8, COLS)))
+    g3 = gather(parts, select_ref[:, :CASE])[0:1]
+    for i, value in enumerate((g1, g2, g3)):
+        part_ref[:, i * CASE : (i + 1) * CASE] = value
 
     x_copies = [
         remote(part_ref, x_in.at[d], x_send.at[d], x_recv.at[d], "bus", x_peers[d])
@@ -249,7 +273,8 @@
         signs_ref[rows, :] = (onehot(ids == start) - onehot(ids == end)).astype(BF16)
         return carry
 
-    lax.fori_loop(0, 3, build_signs, 0)
+    lax.fori_loop(0, BR // CHUNK, build_signs, 0)
+    fault_part(0)
     for copy in x_copies:
         copy.wait_recv()
     total = part_ref[...]
@@ -262,15 +287,16 @@
     ]
     for copy in z_copies:
         copy.start()
-    lax.fori_loop(3, BR // CHUNK, build_signs, 0)
     for copy in halo:
         copy.wait_recv()
-
-    def gather_halo(i, carry):
-        cols_ref[pl.ds(pl.multiple_of(BUS + i * HB, HB), HB), :] = columns_of(rows_in[i])
-        return carry
-
-    lax.fori_loop(0, 2, gather_halo, 0)
+    for copy in hand:
+        copy.start()
+    for i in range(1, BUS // CHUNK):
+        fault_part(i)
+    for copy in hand:
+        copy.wait_recv()
+    parts = pieces(rows_in[...].reshape(2 * HB, COLS))
+    cols_ref[BUS:, :] = gather(parts, select_ref[...])
     for copy in z_copies:
         copy.wait_recv()
     for d in range(n_z - 1):
@@ -287,9 +313,7 @@
         if keep:
             volt_ref[rows, :] = volt
         for j, piece in enumerate(pieces(volt)):
-            for h in range(2):
-                at = (h * 3 + j) * HALF
-                v_ref[rows, at : at + HALF] = piece[:, h * HALF : (h + 1) * HALF]
+            v_ref[rows, j * CASE : (j + 1) * CASE] = piece
 
     @pl.loop(0, BUS // HB)
     def _(i):
@@ -299,23 +323,23 @@
     def _(i):
         finish(i, False)
 
-    for h in range(2):
-        got = jnp.dot(
-            signs_ref[...],
-            v_ref[:, h * 3 * HALF : (h + 1) * 3 * HALF],
-            preferred_element_type=F32,
-        )
-        rate_ref[:, h * HALF : (h + 1) * HALF] = (got[:, :HALF] + got[:, HALF : 2 * HALF]) + got[
-            :, 2 * HALF :
-        ]
-
-    @pl.loop(0, BR // 128)
-    def _(i):
-        drops = jnp.abs(rate_ref[pl.ds(pl.multiple_of(i * 128, 128), 128), :])
-        tops = drops[:, 0:128]
+    for i in range(BR // CHUNK):
+        signs = signs_ref[i * CHUNK : (i + 1) * CHUNK, :]
+        drops = None
+        for j in range(3):
+            term = jnp.dot(
+                signs, v_ref[:, j * CASE : (j + 1) * CASE], preferred_element_type=F32
+            )
+            drops = term if drops is None else drops + term
+        rate_ref[i * CHUNK : (i + 1) * CHUNK, :] = drops
+        sizes = jnp.abs(drops)
+        tops = sizes[:, 0:128]
         for j in range(1, CASE // 128):
-            tops = jnp.maximum(tops, drops[:, j * 128 : (j + 1) * 128])
-        most_ref[pl.ds(i, 1), :] = jnp.max(tops.T, axis=0, keepdims=True)
+            tops = jnp.maximum(tops, sizes[:, j * 128 : (j + 1) * 128])
+        for j in range(CHUNK // 128):
+            at = i * (CHUNK // 128) + j
+            block = tops[j * 128 : (j + 1) * 128].T
+            most_ref[at : at + 1, :] = jnp.max(block, axis=0, keepdims=True)
 
     c_copies = [
         remote(most_ref, most_in.at[d], c_send.at[d], c_recv.at[d], "case", case_peers[d])
@@ -335,12 +359,16 @@
         c_copies[d].wait_recv()
         most = jnp.maximum(most, most_in[d])
     worst_ref[...] = relay_of(most * scale, half, inverse)
-    for copy in halo + x_copies + z_copies + c_copies:
+    for copy in halo + hand + x_copies + z_copies + c_copies:
         copy.wait_send()
 
 
 def store_kernel(volt_ref, rate_ref, worst_ref, volt_hbm, rate_hbm, worst_hbm, sem):
-    pairs = [(volt_ref, volt_hbm), (rate_ref, rate_hbm), (worst_ref, worst_hbm)]
+    pairs = [(worst_ref, worst_hbm)]
+    for src, dst, n in ((rate_ref, rate_hbm, BR), (volt_ref, volt_hbm, BUS)):
+        for i in range(n // CHUNK):
+            rows = pl.ds(i * CHUNK, CHUNK)
+            pairs.append((src.at[rows], dst.at[rows]))
     copies = [pltpu.make_async_copy(src, dst, sem.at[i]) for i, (src, dst) in enumerate(pairs)]
     for copy in copies:
         copy.start()
@@ -406,9 +434,10 @@
             pltpu.VMEM((BR // 128, 128), F32),
             pltpu.VMEM((BR // 128, 128), I32),
             pltpu.VMEM((BUS, COLS), F32),
+            pltpu.VMEM((3, BUS, COLS), BF16),
             pltpu.VMEM((COLS, 2 * CASE), BF16),
             pltpu.VMEM((EXT, 2 * CASE), F32),
-            pltpu.VMEM((2, HB, COLS), F32),
+            pltpu.VMEM((2, HALF, COLS), F32),
             pltpu.VMEM((2, HB, COLS), F32),
             pltpu.VMEM((1, 3 * CASE), F32),
             pltpu.VMEM((1, 3 * CASE), F32),
@@ -421,6 +450,8 @@
             pltpu.VMEM((n_case - 1, BR // 128, 128), F32),
             dma((11,)),
             dma((BUS // CHUNK,)),
+            dma((2,)),
+            dma((2,)),
             dma((2,)),
             dma((2,)),
             dma((n_x - 1,)),
@@ -440,7 +471,7 @@
         out_shape=shapes,
         in_specs=[vmem] * 3,
         out_specs=(hbm,) * 3,
-        scratch_shapes=[dma((3,))],
+        scratch_shapes=[dma((1 + (BR + BUS) // CHUNK,))],
         compiler_params=pltpu.CompilerParams(vmem_limit_bytes=MIB),
         name="store",
     )(*results)

time: 44.5 us -> 40.6 us (0.912)
  Pallas kernels: 43.8 us -> 39.7 us
    pallas_call x1, Pallas kernels: 41.4 us -> 37.2 us  [per_device(): pl.pallas_call(functools.partial(screen_kernel, n_x, n_z, n_case), out_sh...]
where the time goes in v4:
time: 40.6 us; the launch traced here: 40.5 us
  Pallas kernels  39.7 us (98%)
  between operations  0.8 us (2%)
    pallas_call x1, Pallas kernels, per_device(): pl.pallas_call(functools.partial(screen_kernel, n_x, n_z, n_case), out_sh...  37.2 us
    pallas_call x1, Pallas kernels, per_device(): pl.pallas_call(store_kernel, out_shape=shapes, in_specs=[vmem] * 3, out_s...  2.43 us

profile of v4, /device:TPU:1, one launch (start us, length us, event | category | flops | bytes accessed | tf_op | source)
XLA Modules:
  0.0 40.5 jit_solution(12480785194955334412)
XLA Ops:
  0.6 37.2 %screen.1 = (f32[1024,512]{1,0:T(8,128)S(1)}, f32[1536,512]{1,0:T(8,128)S(1)}, f32[12,128]{1,0:T(8,128)S(1)}) custom-call(f32[1024,1024]{1,0:T(8,128)} %z_hbm.1, s32[1,1024]{1,0:T(1,128)} %bitcast.16, s32[1,512]{1,0:T(1,128)} %bitcast.18, s32[2,512]{1,0:T(2,128)} %bitcast.17, f32[1,512]{1,0:T(1,128)} %bitcast.19, f32[1,512]{1,0:T(1,128)} %bitcast.20, ...), custom_call_target="tpu_custom_call" | custom-call | tf_op jit(solution)/shard_map/screen/pallas_call | solution.py:419
  37.9 2.4 %store.1 = (f32[1024,512]{1,0:T(8,128)}, f32[1536,512]{1,0:T(8,128)}, f32[12,128]{1,0:T(8,128)}) custom-call(f32[1024,512]{1,0:T(8,128)S(1)} %get-tuple-element.9.volt_ref, f32[1536,512]{1,0:T(8,128)S(1)} %get-tuple-element.10.rate_ref, f32[12,128]{1,0:T(8,128)S(1)} %get-tuple-element.11.worst_ref), custom_call_target="tpu_custom_call" | custom-call | tf_op jit(solution)/shard_map/store/pallas_call | solution.py:469

commit v5 on v4

--- a/solution.py
+++ b/solution.py
@@ -143,14 +143,13 @@
     fault = fault_ref[...]
     first, second = switch_ref[0:1, :], switch_ref[1:2, :]
 
-    def build(i, carry):
+    def column_rows(i):
         k = lax.broadcasted_iota(I32, (CHUNK, CASE), 0) + i * CHUNK
-        rows = pl.ds(pl.multiple_of(i * CHUNK, CHUNK), CHUNK)
-        select_ref[rows, 0:CASE] = onehot(k == fault).astype(BF16)
+        return slice(i * CHUNK, (i + 1) * CHUNK), k
+
+    for i in range(COLS // CHUNK):
+        rows, k = column_rows(i)
         select_ref[rows, CASE:] = (onehot(k == first) - onehot(k == second)).astype(BF16)
-        return carry
-
-    lax.fori_loop(0, COLS // CHUNK, build, 0)
 
     lists = jnp.where(core == 0, lists_ref[:, :HALF], lists_ref[:, HALF:])
     rim_ids = lax.broadcasted_iota(I32, (RIM, HALF), 0)
@@ -165,6 +164,14 @@
             total = term if total is None else total + term
         rows_out[side] = total
 
+    loads[0].wait()
+    loads[3].wait()
+    boundary(0, 0)
+    boundary(1, BUS - RIM)
+    for i in range(COLS // CHUNK):
+        rows, k = column_rows(i)
+        select_ref[rows, 0:CASE] = onehot(k == fault).astype(BF16)
+
     def remote(src, dst, send, recv, axis, peer):
         return pltpu.make_async_remote_copy(
             src_ref=src,
@@ -175,10 +182,9 @@
             device_id_type=MESH,
         )
 
-    mine = pl.ds(pl.multiple_of(core * HALF, HALF), HALF)
     halo, hand = [], []
     for side, peer in ((0, upper), (1, lower)):
-        part = rows_in.at[side, mine]
+        part = rows_in.at[core, side]
         halo.append(
             remote(
                 rows_out.at[1 - side], part, halo_send.at[side], halo_recv.at[side], "bus", peer
@@ -196,16 +202,16 @@
             total = term if total is None else total + term
         return total
 
-    def switch_part(i, sums):
-        g1, g2, own = sums
-        rows = pl.ds(i * CHUNK, CHUNK)
+    def switch_part(start, size, sums):
+        g1, g2 = sums
+        rows = pl.ds(start, size)
         z = z_ref[rows, :]
         parts = pieces(z)
         for j in range(3):
             cut_ref[j, rows, :] = parts[j]
         diff = gather(parts, select_ref[:, CASE:])
         cols_ref[rows, CASE:] = diff
-        ids = lax.broadcasted_iota(I32, (CHUNK, COLS), 0) + i * CHUNK
+        ids = lax.broadcasted_iota(I32, (size, COLS), 0) + start
         resident = ids == local
         owner = jnp.max(jnp.where(resident, column_ids, -1.0), axis=1, keepdims=True)
         g1 = g1 + jnp.sum(
@@ -214,8 +220,12 @@
             keepdims=True,
         )
         g2 = g2 + jnp.sum(jnp.where(owner == fault_f, diff, 0.0), axis=0, keepdims=True)
-        own = own + jnp.sum(jnp.where(resident, z, 0.0), axis=0, keepdims=True)
-        return g1, g2, own
+        return g1, g2
+
+    def own_part(start, size):
+        ids = lax.broadcasted_iota(I32, (size, COLS), 0) + start
+        z = z_ref[pl.ds(start, size), :]
+        return jnp.sum(jnp.where(ids == local, z, 0.0), axis=0, keepdims=True)
 
     def fault_part(i):
         rows = pl.ds(i * CHUNK, CHUNK)
@@ -223,22 +233,21 @@
         cols_ref[rows, :CASE] = gather(parts, select_ref[:, :CASE])
 
     zero = jnp.zeros((1, CASE), F32)
-    sums = (zero, zero, jnp.zeros((1, COLS), F32))
-    loads[0].wait()
-    loads[3].wait()
-    boundary(0, 0)
-    boundary(1, BUS - RIM)
-    sums = switch_part(0, sums)
+    sums = (zero, zero)
+    sums = switch_part(0, 128, sums)
     pl.semaphore_wait(barrier, len(bus_peers) + len(case_peers))
     for copy in halo:
         copy.start()
     loads[1].wait()
     loads[2].wait()
-    for i in (3, 1, 2):
-        sums = switch_part(i, sums)
-    g1, g2, own = sums
+    own = own_part(0, 128)
+    for start, size in ((128, 128), (768, 256), (256, 256)):
+        sums = switch_part(start, size, sums)
+        own = own + own_part(start, size)
+    own = own + own_part(512, 256)
     parts = pieces(jnp.broadcast_to(own, (8, COLS)))
     g3 = gather(parts, select_ref[:, :CASE])[0:1]
+    g1, g2 = switch_part(512, 256, sums)
     for i, value in enumerate((g1, g2, g3)):
         part_ref[:, i * CASE : (i + 1) * CASE] = value
 
@@ -265,16 +274,16 @@
     rows = jnp.concatenate(rows + [jnp.zeros((3, BR), F32)], axis=0)
     par_ref[...] = rows.T
 
-    def build_signs(i, carry):
-        rows = pl.ds(pl.multiple_of(i * CHUNK, CHUNK), CHUNK)
+    def build_signs(i):
+        rows = pl.ds(i * CHUNK, CHUNK)
         par = par_ref[rows, :]
         ids = lax.broadcasted_iota(I32, (CHUNK, EXT), 1)
         start, end = par[:, 0:1].astype(I32), par[:, 1:2].astype(I32)
         signs_ref[rows, :] = (onehot(ids == start) - onehot(ids == end)).astype(BF16)
-        return carry
-
-    lax.fori_loop(0, BR // CHUNK, build_signs, 0)
+
     fault_part(0)
+    build_signs(0)
+    build_signs(1)
     for copy in x_copies:
         copy.wait_recv()
     total = part_ref[...]
@@ -287,16 +296,29 @@
     ]
     for copy in z_copies:
         copy.start()
+    fault_part(1)
+    build_signs(2)
+    build_signs(3)
+
+    def halo_part(half):
+        parts = pieces(rows_in[half].reshape(HB, COLS))
+        got = gather(parts, select_ref[...])
+        for side in range(2):
+            at = pl.multiple_of(BUS + side * HB + half * HALF, HALF)
+            cols_ref[pl.ds(at, HALF), :] = got[side * HALF : (side + 1) * HALF]
+
     for copy in halo:
         copy.wait_recv()
     for copy in hand:
         copy.start()
-    for i in range(1, BUS // CHUNK):
-        fault_part(i)
+    halo_part(core)
+    fault_part(2)
+    build_signs(4)
+    fault_part(3)
+    build_signs(5)
     for copy in hand:
         copy.wait_recv()
-    parts = pieces(rows_in[...].reshape(2 * HB, COLS))
-    cols_ref[BUS:, :] = gather(parts, select_ref[...])
+    halo_part(1 - core)
     for copy in z_copies:
         copy.wait_recv()
     for d in range(n_z - 1):
@@ -306,22 +328,13 @@
     self_z = g3 - g2 * ratio
     amps = 1.0 / (self_z + fault_z_ref[...])
 
-    def finish(i, keep):
-        rows = pl.ds(pl.multiple_of(i * HB, HB), HB)
-        got = cols_ref[rows, :]
-        volt = 1.0 - (got[:, :CASE] - got[:, CASE:] * ratio) * amps
-        if keep:
+    for i in range(EXT // HB):
+        rows = slice(i * HB, (i + 1) * HB)
+        volt = 1.0 - (cols_ref[rows, :CASE] - cols_ref[rows, CASE:] * ratio) * amps
+        if i < BUS // HB:
             volt_ref[rows, :] = volt
         for j, piece in enumerate(pieces(volt)):
             v_ref[rows, j * CASE : (j + 1) * CASE] = piece
-
-    @pl.loop(0, BUS // HB)
-    def _(i):
-        finish(i, True)
-
-    @pl.loop(BUS // HB, EXT // HB)
-    def _(i):
-        finish(i, False)
 
     for i in range(BR // CHUNK):
         signs = signs_ref[i * CHUNK : (i + 1) * CHUNK, :]
@@ -438,7 +451,7 @@
             pltpu.VMEM((COLS, 2 * CASE), BF16),
             pltpu.VMEM((EXT, 2 * CASE), F32),
             pltpu.VMEM((2, HALF, COLS), F32),
-            pltpu.VMEM((2, HB, COLS), F32),
+            pltpu.VMEM((2, 2, HALF, COLS), F32),
             pltpu.VMEM((1, 3 * CASE), F32),
             pltpu.VMEM((1, 3 * CASE), F32),
             pltpu.VMEM((n_x - 1, 1, 3 * CASE), F32),

time: 40.6 us -> 40.3 us (level)
  no operation moved by 1% of the time
where the time goes in v5:
time: 40.3 us; the launch traced here: 40.2 us
  Pallas kernels  39.4 us (98%)
  between operations  0.8 us (2%)
    pallas_call x1, Pallas kernels, per_device(): pl.pallas_call(functools.partial(screen_kernel, n_x, n_z, n_case), out_sh...  37 us
    pallas_call x1, Pallas kernels, per_device(): pl.pallas_call(store_kernel, out_shape=shapes, in_specs=[vmem] * 3, out_s...  2.43 us

profile of v5, /device:TPU:1, one launch (start us, length us, event | category | flops | bytes accessed | tf_op | source)
XLA Modules:
  0.0 40.2 jit_solution(14034561850222987367)
XLA Ops:
  0.6 37.0 %screen.1 = (f32[1024,512]{1,0:T(8,128)S(1)}, f32[1536,512]{1,0:T(8,128)S(1)}, f32[12,128]{1,0:T(8,128)S(1)}) custom-call(f32[1024,1024]{1,0:T(8,128)} %z_hbm.1, s32[1,1024]{1,0:T(1,128)} %bitcast.16, s32[1,512]{1,0:T(1,128)} %bitcast.18, s32[2,512]{1,0:T(2,128)} %bitcast.17, f32[1,512]{1,0:T(1,128)} %bitcast.19, f32[1,512]{1,0:T(1,128)} %bitcast.20, ...), custom_call_target="tpu_custom_call" | custom-call | tf_op jit(solution)/shard_map/screen/pallas_call | solution.py:432
  37.6 2.4 %store.1 = (f32[1024,512]{1,0:T(8,128)}, f32[1536,512]{1,0:T(8,128)}, f32[12,128]{1,0:T(8,128)}) custom-call(f32[1024,512]{1,0:T(8,128)S(1)} %get-tuple-element.9.volt_ref, f32[1536,512]{1,0:T(8,128)S(1)} %get-tuple-element.10.rate_ref, f32[12,128]{1,0:T(8,128)S(1)} %get-tuple-element.11.worst_ref), custom_call_target="tpu_custom_call" | custom-call | tf_op jit(solution)/shard_map/store/pallas_call | solution.py:482

commit v6 on v5

--- a/solution.py
+++ b/solution.py
@@ -25,6 +25,10 @@
 
 def in_hbm(value):
     return pltpu.with_memory_space_constraint(value, pltpu.HBM)
+
+
+def farthest_first(n):
+    return sorted(range(1, n), key=lambda d: (-min(d, n - d), d))
 
 
 def onehot(mask):
@@ -98,11 +102,11 @@
     bus, case = lax.axis_index("bus"), lax.axis_index("case")
     my_x, my_z = bus // n_z, bus % n_z
     upper, lower = (bus + 1) % n_bus, (bus + n_bus - 1) % n_bus
-    x_peers = [((my_x + d) % n_x) * n_z + my_z for d in range(1, n_x)]
-    z_peers = [my_x * n_z + (my_z + d) % n_z for d in range(1, n_z)]
+    x_peers = [((my_x + d) % n_x) * n_z + my_z for d in farthest_first(n_x)]
+    z_peers = [my_x * n_z + (my_z + d) % n_z for d in farthest_first(n_z)]
     core = case % 2
     sibling = case + 1 - 2 * core
-    case_peers = [(case + d) % n_case for d in range(1, n_case)]
+    case_peers = [(case + d) % n_case for d in farthest_first(n_case)]
 
     small = [
         (fault_hbm, fault_ref),

time: 40.3 us -> 40.1 us (level)
  no operation moved by 1% of the time
where the time goes in v6:
time: 40.1 us; the launch traced here: 40 us
  Pallas kernels  39.2 us (98%)
  between operations  0.8 us (2%)
    pallas_call x1, Pallas kernels, per_device(): pl.pallas_call(functools.partial(screen_kernel, n_x, n_z, n_case), out_sh...  36.8 us
    pallas_call x1, Pallas kernels, per_device(): pl.pallas_call(store_kernel, out_shape=shapes, in_specs=[vmem] * 3, out_s...  2.43 us

profile of v6, /device:TPU:1, one launch (start us, length us, event | category | flops | bytes accessed | tf_op | source)
XLA Modules:
  0.0 40.0 jit_solution(1870348250730274202)
XLA Ops:
  0.6 36.8 %screen.1 = (f32[1024,512]{1,0:T(8,128)S(1)}, f32[1536,512]{1,0:T(8,128)S(1)}, f32[12,128]{1,0:T(8,128)S(1)}) custom-call(f32[1024,1024]{1,0:T(8,128)} %z_hbm.1, s32[1,1024]{1,0:T(1,128)} %bitcast.16, s32[1,512]{1,0:T(1,128)} %bitcast.18, s32[2,512]{1,0:T(2,128)} %bitcast.17, f32[1,512]{1,0:T(1,128)} %bitcast.19, f32[1,512]{1,0:T(1,128)} %bitcast.20, ...), custom_call_target="tpu_custom_call" | custom-call | tf_op jit(solution)/shard_map/screen/pallas_call | solution.py:436
  37.4 2.4 %store.1 = (f32[1024,512]{1,0:T(8,128)}, f32[1536,512]{1,0:T(8,128)}, f32[12,128]{1,0:T(8,128)}) custom-call(f32[1024,512]{1,0:T(8,128)S(1)} %get-tuple-element.9.volt_ref, f32[1536,512]{1,0:T(8,128)S(1)} %get-tuple-element.10.rate_ref, f32[12,128]{1,0:T(8,128)S(1)} %get-tuple-element.11.worst_ref), custom_call_target="tpu_custom_call" | custom-call | tf_op jit(solution)/shard_map/store/pallas_call | solution.py:486
